TPU v7x, 32 devices: a whole 2x2x4 slice. The times are simulated.
32 devices in a mesh: seq: 8 (over y, x, core), ffn: 4 (over z).
Axes of the slice: x: 2, y: 2, z: 4, core: 2. Of those that a mesh axis runs over, the one named last changes fastest.
Arguments:
- attn_in: float32 [1024, 2, 1024], P('seq', None, 'ffn'), may hold values from -0.25 to 0.25
- attn_out: float32 [1024, 1024], P('ffn', 'seq'), may hold values from -0.5 to 0.5
- ffn_in: float32 [1024, 4096], P('seq', 'ffn'), may hold values from -0.1875 to 0.1875
- ffn_out: float32 [4096, 1024], P('ffn', 'seq'), may hold values from -0.09375 to 0.09375
- tables: float32 [672, 1024], P(None, ('seq', 'ffn'))
- norm_params: float32 [6, 1024], P(None, ('seq', 'ffn'))
- m_attn_in: float32 [1024, 2, 1024], P('seq', None, 'ffn'), may hold values from -2.2888184e-05 to 2.2888184e-05
- m_attn_out: float32 [1024, 1024], P('ffn', 'seq'), may hold values from -2.2888184e-05 to 2.2888184e-05
- m_ffn_in: float32 [1024, 4096], P('seq', 'ffn'), may hold values from -2.2888184e-05 to 2.2888184e-05
- m_ffn_out: float32 [4096, 1024], P('ffn', 'seq'), may hold values from -2.2888184e-05 to 2.2888184e-05
- m_tables: float32 [672, 1024], P(None, ('seq', 'ffn')), may hold values from -2.2888184e-05 to 2.2888184e-05
- m_norm_params: float32 [6, 1024], P(None, ('seq', 'ffn')), may hold values from -2.2888184e-05 to 2.2888184e-05
- v_attn_in: float32 [1024, 2, 1024], P('seq', None, 'ffn'), may hold values from 2.1674416e-13 to 8.6697663e-13
- v_attn_out: float32 [1024, 1024], P('ffn', 'seq'), may hold values from 2.1674416e-13 to 8.6697663e-13
- v_ffn_in: float32 [1024, 4096], P('seq', 'ffn'), may hold values from 2.1674416e-13 to 8.6697663e-13
- v_ffn_out: float32 [4096, 1024], P('ffn', 'seq'), may hold values from 2.1674416e-13 to 8.6697663e-13
- v_tables: float32 [672, 1024], P(None, ('seq', 'ffn')), may hold values from 2.1674416e-13 to 8.6697663e-13
- v_norm_params: float32 [6, 1024], P(None, ('seq', 'ffn')), may hold values from 2.1674416e-13 to 8.6697663e-13
- tokens: int32 [2, 4096], P(None, 'seq'), may hold values from 0 to 255
- targets: int32 [2, 4096], P(None, ('seq', 'ffn')), may hold values from 0 to 255
- loss_mask: int32 [2, 4096], replicated, may hold values from 0 to 1, as said below
- lengths: int32 [2], replicated, may hold values from 1024 to 4096, as said below
- buckets: int32 [2, 2, 4096, 1], replicated, may hold values from 0 to 255; in each aligned block of 512 rows (0 to 511, 512 to 1023, ..., all dimensions but the last counted through in order) at most 4 rows name the same one
Outputs:
- new_attn_in: float32 [1024, 2, 1024], P('seq', None, 'ffn')
- new_attn_out: float32 [1024, 1024], P('ffn', 'seq')
- new_ffn_in: float32 [1024, 4096], P('seq', 'ffn')
- new_ffn_out: float32 [4096, 1024], P('ffn', 'seq')
- new_tables: float32 [672, 1024], P(None, ('seq', 'ffn'))
- new_norm_params: float32 [6, 1024], P(None, ('seq', 'ffn'))
- new_m_attn_in: float32 [1024, 2, 1024], P('seq', None, 'ffn')
- new_m_attn_out: float32 [1024, 1024], P('ffn', 'seq')
- new_m_ffn_in: float32 [1024, 4096], P('seq', 'ffn')
- new_m_ffn_out: float32 [4096, 1024], P('ffn', 'seq')
- new_m_tables: float32 [672, 1024], P(None, ('seq', 'ffn'))
- new_m_norm_params: float32 [6, 1024], P(None, ('seq', 'ffn'))
- new_v_attn_in: float32 [1024, 2, 1024], P('seq', None, 'ffn')
- new_v_attn_out: float32 [1024, 1024], P('ffn', 'seq')
- new_v_ffn_in: float32 [1024, 4096], P('seq', 'ffn')
- new_v_ffn_out: float32 [4096, 1024], P('ffn', 'seq')
- new_v_tables: float32 [672, 1024], P(None, ('seq', 'ffn'))
- new_v_norm_params: float32 [6, 1024], P(None, ('seq', 'ffn'))
- grad_norm: float32 [], replicated
- loss_total: float32 [], replicated
Inputs may be any that keep to these rules, and one draw needn't show every extreme that they name: `buckets`: in each aligned block of 512 positions of one sequence and one round, no bucket is named more than 4 times, a bound that some block reaches. `lengths`: one sequence of every draw has the full length 4096. `loss_mask`: position 0 of every sequence counts.
All inputs are finite; a program needn't handle non-finite values.
Results may differ from a plain program's by a relative error of at most 0.017.
Values may be sent and summed in bfloat16 or wider, within the bound.
No kernel may reach another device: no remote copies, remote signals or barrier semaphores. Data moves between devices by JAX's collectives and lax.ppermute only.
A program may use at most 192 MiB of HBM per device.

v0:
```python
import jax
import jax.numpy as jnp
from jax import lax
from jax.sharding import PartitionSpec as P

HEAD = 128
VOCAB = 256
BUCKETS = 256
CAP = 4
POS_LO = 128
STEP = 10


PENALTY = 10000.0
MASKED = -1000000000.0
LN_EPS = 1e-05
KEY_EPS = 1e-06
CLIP_NORM = 0.05
BETA_ONE = 0.9
BETA_TWO = 0.999
ADAM_EPS = 1e-08
WEIGHT_DECAY = 0.01
STEP_RATES = (0.1, 0.2, 0.1, 0.05, 0.5, 0.5)
LOG_TWO = 0.6931471805599453


def norm_forward(values, scale_row, shift_row):
    average = jnp.mean(values, axis=-1, keepdims=True)
    centred = values - average
    inv_std = lax.rsqrt(jnp.mean(centred * centred, axis=-1, keepdims=True) + LN_EPS)
    normal_part = centred * inv_std
    return (normal_part * scale_row + shift_row, normal_part, inv_std)


def norm_backward(upstream, normal_part, inv_std, scale_row):
    axes_list = tuple(range(upstream.ndim - 1))
    grad_scale = jnp.sum(upstream * normal_part, axis=axes_list)
    grad_shift = jnp.sum(upstream, axis=axes_list)
    scaled = upstream * scale_row
    grad_input = inv_std * (
        scaled
        - jnp.mean(scaled, axis=-1, keepdims=True)
        - normal_part * jnp.mean(scaled * normal_part, axis=-1, keepdims=True)
    )
    return (grad_input, grad_scale, grad_shift)


def adam_step(weight, grad_value, moment_one, moment_two, step_rate, clip_scale):
    clipped = grad_value * clip_scale
    new_one = BETA_ONE * moment_one + (1.0 - BETA_ONE) * clipped
    new_two = BETA_TWO * moment_two + (1.0 - BETA_TWO) * clipped * clipped
    fix_one = 1.0 - BETA_ONE**STEP
    fix_two = 1.0 - BETA_TWO**STEP
    change = new_one / fix_one / (jnp.sqrt(new_two / fix_two) + ADAM_EPS) + WEIGHT_DECAY * weight
    return (weight - step_rate * change, new_one, new_two)


def share_rows(values):
    return lax.psum_scatter(
        values.astype(jnp.bfloat16), "ffn", scatter_dimension=1, tiled=True
    ).astype(jnp.float32)


def whole_rows(values):
    return lax.all_gather(values, "ffn", axis=1, tiled=True)


def total_rows(values):
    return lax.psum(values.astype(jnp.bfloat16), "ffn").astype(jnp.float32)


def into_slots(payload, slot_index, total_slots, n_seq):
    num_seqs, num_rounds = (payload.shape[0], payload.shape[1])
    seq_index = jnp.arange(num_seqs, dtype=jnp.int32)[:, None, None]
    round_index = jnp.arange(num_rounds, dtype=jnp.int32)[None, :, None]
    buffer = jnp.zeros((num_seqs, num_rounds, total_slots, payload.shape[-1]), payload.dtype)
    buffer = buffer.at[seq_index, round_index, slot_index].set(payload)
    return buffer.reshape(num_seqs, num_rounds, n_seq, total_slots // n_seq, payload.shape[-1])


def from_slots(arrived, slot_index):
    shape = arrived.shape
    flat_rows = arrived.reshape(shape[0], shape[1], shape[2] * shape[3], shape[4])
    return jnp.take_along_axis(flat_rows, slot_index[..., None], axis=2)


def by_bucket(arrived, capacity):
    shape = arrived.shape
    per_dev = shape[3] // capacity
    grouped = arrived.reshape(shape[0], shape[1], shape[2], per_dev, capacity, shape[4])
    return grouped.transpose(0, 1, 3, 2, 4, 5).reshape(
        shape[0], shape[1], per_dev, shape[2] * capacity, shape[4]
    )


def by_source(values, n_seq, capacity):
    shape = values.shape
    grouped = values.reshape(shape[0], shape[1], shape[2], n_seq, capacity, shape[4])
    return grouped.transpose(0, 1, 3, 2, 4, 5).reshape(
        shape[0], shape[1], n_seq, shape[2] * capacity, shape[4]
    )


def owner_scores(rows, slot_pos, lengths, head_size):
    half_width = rows.shape[-1] // 2
    leading = rows.shape[:4]
    queries = rows[..., :half_width].reshape(leading + (half_width // head_size, head_size))
    values = rows[..., half_width:].reshape(leading + (half_width // head_size, head_size))
    widened = queries.astype(jnp.float32)
    inv_norm = lax.rsqrt(jnp.sum(widened * widened, axis=-1, keepdims=True) + KEY_EPS)
    unit_keys = (widened * inv_norm).astype(jnp.bfloat16)
    raw_scores = jnp.einsum(
        "srbihc,srbjhc->srbhij", queries, unit_keys, preferred_element_type=jnp.float32
    )
    query_pos = slot_pos[:, :, :, None, :, None]
    key_pos = slot_pos[:, :, :, None, None, :]
    seq_limit = lengths[:, None, None, None, None, None]
    allowed = (key_pos < query_pos) & (key_pos >= 0) & (key_pos < seq_limit)
    slot_count = slot_pos.shape[-1]
    diagonal = jnp.arange(slot_count)[:, None] == jnp.arange(slot_count)[None, :]
    scores = jnp.where(allowed, raw_scores, jnp.where(diagonal, raw_scores - PENALTY, MASKED))
    return (queries, values, unit_keys, widened, inv_norm, scores)


def per_device(
    attn_in,
    attn_out,
    ffn_in,
    ffn_out,
    tables,
    norm_params,
    m_attn_in,
    m_attn_out,
    m_ffn_in,
    m_ffn_out,
    m_tables,
    m_norm_params,
    v_attn_in,
    v_attn_out,
    v_ffn_in,
    v_ffn_out,
    v_tables,
    v_norm_params,
    tokens,
    targets,
    loss_mask,
    lengths,
    buckets,
):
    n_seq = lax.axis_size("seq")
    seq_rank = lax.axis_index("seq")
    ffn_rank = lax.axis_index("ffn")
    num_seqs, seg_len = tokens.shape
    sub_len = targets.shape[1]
    full_len = loss_mask.shape[1]
    num_rounds = buckets.shape[1]
    per_dev = BUCKETS // n_seq
    total_slots = BUCKETS * CAP
    upper_rows = full_len // POS_LO
    w_in, w_out, w_up, w_down = (
        lax.all_gather(attn_in.astype(jnp.bfloat16), "seq", axis=0, tiled=True),
        lax.all_gather(attn_out.astype(jnp.bfloat16), "seq", axis=1, tiled=True),
        lax.all_gather(ffn_in.astype(jnp.bfloat16), "seq", axis=0, tiled=True),
        lax.all_gather(ffn_out.astype(jnp.bfloat16), "seq", axis=1, tiled=True),
    )
    table_all, norm_all = (
        lax.all_gather(tables.astype(jnp.bfloat16), ("seq", "ffn"), axis=1, tiled=True),
        lax.all_gather(norm_params.astype(jnp.bfloat16), ("seq", "ffn"), axis=1, tiled=True),
    )
    norm_rows = norm_all.astype(jnp.float32)
    head_width = w_in.shape[2]
    heads_local = head_width // HEAD
    seg_start = seq_rank * seg_len
    position = seg_start + jnp.arange(seg_len, dtype=jnp.int32)
    embedded = table_all[tokens].astype(jnp.float32)
    embedded = embedded + table_all[2 * VOCAB + position // POS_LO].astype(jnp.float32)[None]
    embedded = (
        embedded + table_all[2 * VOCAB + upper_rows + position % POS_LO].astype(jnp.float32)[None]
    )
    normed_full, normal_one, inv_one = norm_forward(embedded, norm_rows[0], norm_rows[1])
    normed = normed_full.astype(jnp.bfloat16)
    projected = jnp.einsum("std,dkc->stkc", normed, w_in, preferred_element_type=jnp.float32)
    payload = projected.astype(jnp.bfloat16).reshape(num_seqs, seg_len, 2 * head_width)
    own_ids = lax.dynamic_slice_in_dim(buckets[..., 0], seg_start, seg_len, 2)
    one_hot = (own_ids[..., None] == jnp.arange(BUCKETS, dtype=jnp.int32)).astype(jnp.int32)
    own_rank = jnp.sum(jnp.cumsum(one_hot, axis=2) * one_hot, axis=-1) - 1
    slot_index = own_ids * CAP + own_rank
    spread = jnp.broadcast_to(payload[:, None], (num_seqs, num_rounds, seg_len, 2 * head_width))
    arrived = lax.all_to_all(
        into_slots(spread, slot_index, total_slots, n_seq),
        "seq",
        split_axis=2,
        concat_axis=2,
        tiled=True,
    )
    rows_kept = by_bucket(arrived, CAP)
    ids_all = buckets[..., 0].reshape(num_seqs, num_rounds, n_seq, seg_len)
    owned = seq_rank * per_dev + jnp.arange(per_dev, dtype=jnp.int32)
    occupied = (ids_all[..., None] == owned).astype(jnp.int32)
    ranking = jnp.cumsum(occupied, axis=3) - 1
    global_pos = (
        jnp.arange(n_seq, dtype=jnp.int32)[:, None] * seg_len
        + jnp.arange(seg_len, dtype=jnp.int32)[None, :]
    )[:, :, None] + 1
    columns = []
    for column in range(CAP):
        columns.append(jnp.sum(occupied * (ranking == column) * global_pos, axis=3) - 1)
    slot_pos = (
        jnp.stack(columns, axis=-1)
        .transpose(0, 1, 3, 2, 4)
        .reshape(num_seqs, num_rounds, per_dev, n_seq * CAP)
    )
    queries, values, unit_keys, widened, inv_norm, scores = owner_scores(
        rows_kept, slot_pos, lengths, HEAD
    )
    owner_total = jax.nn.logsumexp(scores, axis=-1)
    probability = jnp.exp(scores - owner_total[..., None])
    result = jnp.einsum(
        "srbhij,srbjhc->srbihc",
        probability.astype(jnp.bfloat16),
        values,
        preferred_element_type=jnp.float32,
    )
    result = result.reshape(result.shape[:4] + (head_width,))
    owner_lse = owner_total.transpose(0, 1, 2, 4, 3)
    back_out, back_lse = (
        lax.all_to_all(
            by_source(result, n_seq, CAP).astype(jnp.bfloat16),
            "seq",
            split_axis=2,
            concat_axis=2,
            tiled=True,
        ).astype(jnp.float32),
        lax.all_to_all(
            by_source(owner_lse, n_seq, CAP).astype(jnp.bfloat16),
            "seq",
            split_axis=2,
            concat_axis=2,
            tiled=True,
        ).astype(jnp.float32),
    )
    round_out = from_slots(back_out, slot_index)
    round_lse = from_slots(back_lse, slot_index)
    mixing = jax.nn.softmax(round_lse, axis=1)
    round_heads = round_out.reshape(num_seqs, num_rounds, seg_len, heads_local, HEAD)
    attended = jnp.sum(mixing[..., None] * round_heads, axis=1).reshape(
        num_seqs, seg_len, head_width
    )
    attended = attended.astype(jnp.bfloat16)
    branch = jnp.einsum("stc,cd->std", attended, w_out, preferred_element_type=jnp.float32)
    sub_start = ffn_rank * sub_len
    own_embed = lax.dynamic_slice_in_dim(embedded, sub_start, sub_len, 1)
    first_out = embedded + total_rows(branch)
    middle_full, normal_two, inv_two = norm_forward(first_out, norm_rows[2], norm_rows[3])
    middle = middle_full.astype(jnp.bfloat16)
    own_first = lax.dynamic_slice_in_dim(first_out, sub_start, sub_len, 1)
    pre_act = jnp.einsum("std,df->stf", middle, w_up, preferred_element_type=jnp.float32)
    hidden = jnp.maximum(pre_act, 0.0).astype(jnp.bfloat16)
    ffn_part = jnp.einsum("stf,fd->std", hidden, w_down, preferred_element_type=jnp.float32)
    second_add = share_rows(ffn_part)
    second_out = own_embed + second_add
    final_full, normal_three, inv_three = norm_forward(
        own_first + second_out, norm_rows[4], norm_rows[5]
    )
    final_rows = final_full.astype(jnp.bfloat16)
    head_rows = table_all[VOCAB : 2 * VOCAB]
    logits = jnp.einsum("std,vd->stv", final_rows, head_rows, preferred_element_type=jnp.float32)
    log_norm = jax.nn.logsumexp(logits, axis=-1)
    target_hot = (targets[..., None] == jnp.arange(VOCAB, dtype=jnp.int32)).astype(jnp.float32)
    picked = jnp.sum(logits * target_hot, axis=-1)
    bits_lost = (log_norm - picked) / LOG_TWO
    live_all = (
        loss_mask * (jnp.arange(full_len, dtype=jnp.int32)[None, :] < lengths[:, None])
    ).astype(jnp.float32)
    counts = jnp.sum(live_all, axis=1)
    live_own = lax.dynamic_slice_in_dim(live_all, seg_start + sub_start, sub_len, 1)
    weight_row = lengths.astype(jnp.float32) / full_len / counts
    loss_weight = live_own * weight_row[:, None]
    loss_part = jnp.sum(loss_weight * bits_lost)
    softmax_p = jnp.exp(logits - log_norm[..., None])
    grad_logits = ((loss_weight / LOG_TWO)[..., None] * (softmax_p - target_hot)).astype(
        jnp.bfloat16
    )
    grad_final = jnp.einsum(
        "stv,vd->std", grad_logits, head_rows, preferred_element_type=jnp.float32
    )
    grad_head = jnp.einsum(
        "stv,std->vd", grad_logits, final_rows, preferred_element_type=jnp.float32
    )
    grad_sum, gain_five, bias_five = norm_backward(
        grad_final, normal_three, inv_three, norm_rows[4]
    )
    rows_grad = whole_rows(grad_sum.astype(jnp.bfloat16))
    grad_hidden = jnp.einsum("std,fd->stf", rows_grad, w_down, preferred_element_type=jnp.float32)
    grad_pre = jnp.where(pre_act > 0.0, grad_hidden, 0.0).astype(jnp.bfloat16)
    grad_down = jnp.einsum("stf,std->fd", hidden, rows_grad, preferred_element_type=jnp.float32)
    grad_up = jnp.einsum("std,stf->df", middle, grad_pre, preferred_element_type=jnp.float32)
    grad_middle = jnp.einsum("stf,df->std", grad_pre, w_up, preferred_element_type=jnp.float32)
    first_part, gain_three, bias_three = norm_backward(
        grad_middle, normal_two, inv_two, norm_rows[2]
    )
    own_part = lax.dynamic_slice_in_dim(first_part, sub_start, sub_len, 1) + grad_sum
    first_part = lax.dynamic_update_slice_in_dim(first_part, own_part, sub_start, 1)
    grad_first = total_rows(first_part)
    grad_first_own = lax.dynamic_slice_in_dim(grad_first, sub_start, sub_len, 1)
    grad_branch = grad_first.astype(jnp.bfloat16)
    grad_out = jnp.einsum("stc,std->cd", attended, grad_branch, preferred_element_type=jnp.float32)
    grad_att = jnp.einsum("std,cd->stc", grad_branch, w_out, preferred_element_type=jnp.float32)
    grad_att = lax.optimization_barrier(grad_att.astype(jnp.bfloat16)).astype(jnp.float32)
    grad_att = grad_att.reshape(num_seqs, 1, seg_len, heads_local, HEAD)
    grad_mix = jnp.sum(grad_att * round_heads, axis=-1)
    grad_total = mixing * (grad_mix - jnp.sum(mixing * grad_mix, axis=1, keepdims=True))
    grad_round = (mixing[..., None] * grad_att).astype(jnp.bfloat16)
    grad_round = grad_round.reshape(num_seqs, num_rounds, seg_len, head_width)
    send_rows = jnp.concatenate([grad_round, spread], axis=-1)
    arrived_grad = lax.all_to_all(
        into_slots(send_rows, slot_index, total_slots, n_seq),
        "seq",
        split_axis=2,
        concat_axis=2,
        tiled=True,
    )
    arrived_total = lax.all_to_all(
        into_slots(grad_total, slot_index, total_slots, n_seq),
        "seq",
        split_axis=2,
        concat_axis=2,
        tiled=True,
    )
    grad_rows_owner = by_bucket(arrived_grad, CAP)
    grad_owner_total = by_bucket(arrived_total, CAP).transpose(0, 1, 2, 4, 3)
    rows_again = grad_rows_owner[..., head_width:]
    queries, values, unit_keys, widened, inv_norm, scores = owner_scores(
        rows_again, slot_pos, lengths, HEAD
    )
    probability = jnp.exp(scores - owner_total[..., None])
    leading = grad_rows_owner.shape[:4]
    grad_result = grad_rows_owner[..., :head_width].reshape(leading + (heads_local, HEAD))
    grad_p = jnp.einsum(
        "srbihc,srbjhc->srbhij", grad_result, values, preferred_element_type=jnp.float32
    )
    grad_values = jnp.einsum(
        "srbhij,srbihc->srbjhc",
        probability.astype(jnp.bfloat16),
        grad_result,
        preferred_element_type=jnp.float32,
    )
    inner = jnp.sum(probability * grad_p, axis=-1, keepdims=True)
    grad_scores = (probability * (grad_p - inner + grad_owner_total[..., None])).astype(
        jnp.bfloat16
    )
    grad_queries = jnp.einsum(
        "srbhij,srbjhc->srbihc", grad_scores, unit_keys, preferred_element_type=jnp.float32
    )
    grad_keys = jnp.einsum(
        "srbhij,srbihc->srbjhc", grad_scores, queries, preferred_element_type=jnp.float32
    )
    grad_qk = (
        grad_queries
        + grad_keys * inv_norm
        - widened * inv_norm**3 * jnp.sum(widened * grad_keys, axis=-1, keepdims=True)
    )
    owner_grads = jnp.concatenate(
        [grad_qk.reshape(leading + (head_width,)), grad_values.reshape(leading + (head_width,))],
        axis=-1,
    )
    returned = lax.all_to_all(
        by_source(owner_grads, n_seq, CAP).astype(jnp.bfloat16),
        "seq",
        split_axis=2,
        concat_axis=2,
        tiled=True,
    ).astype(jnp.float32)
    token_grads = jnp.sum(from_slots(returned, slot_index), axis=1).astype(jnp.bfloat16)
    grad_proj = token_grads.reshape(num_seqs, seg_len, 2, head_width)
    grad_in = jnp.einsum("std,stkc->dkc", normed, grad_proj, preferred_element_type=jnp.float32)
    grad_normed = jnp.einsum("stkc,dkc->std", grad_proj, w_in, preferred_element_type=jnp.float32)
    embed_part, gain_one, bias_one = norm_backward(grad_normed, normal_one, inv_one, norm_rows[0])
    own_embed_grad = (
        lax.dynamic_slice_in_dim(embed_part, sub_start, sub_len, 1) + grad_first_own + grad_sum
    )
    embed_grad = lax.dynamic_update_slice_in_dim(embed_part, own_embed_grad, sub_start, 1)
    grad_embed = jax.ops.segment_sum(
        embed_grad.reshape(num_seqs * seg_len, -1), tokens.reshape(-1), VOCAB
    )
    pos_grad = jnp.sum(embed_grad, axis=0)
    grad_upper = jax.ops.segment_sum(pos_grad, position // POS_LO, upper_rows)
    grad_lower = jax.ops.segment_sum(pos_grad, position % POS_LO, POS_LO)
    grad_tables = jnp.concatenate([grad_embed, grad_head, grad_upper, grad_lower], axis=0)
    grad_norms = jnp.stack([gain_one, bias_one, gain_three, bias_three, gain_five, bias_five])
    table_grad, norm_grad = (
        lax.psum_scatter(grad_tables, ("seq", "ffn"), scatter_dimension=1, tiled=True),
        lax.psum_scatter(grad_norms, ("seq", "ffn"), scatter_dimension=1, tiled=True),
    )
    in_grad, out_grad, up_grad, down_grad = (
        lax.psum_scatter(
            grad_in.astype(jnp.bfloat16), "seq", scatter_dimension=0, tiled=True
        ).astype(jnp.float32),
        lax.psum_scatter(
            grad_out.astype(jnp.bfloat16), "seq", scatter_dimension=1, tiled=True
        ).astype(jnp.float32),
        lax.psum_scatter(
            grad_up.astype(jnp.bfloat16), "seq", scatter_dimension=0, tiled=True
        ).astype(jnp.float32),
        lax.psum_scatter(
            grad_down.astype(jnp.bfloat16), "seq", scatter_dimension=1, tiled=True
        ).astype(jnp.float32),
    )
    grad_list = (in_grad, out_grad, up_grad, down_grad, table_grad, norm_grad)
    local_sq = jnp.float32(0.0)
    for grad_piece in grad_list:
        local_sq = local_sq + jnp.sum(grad_piece * grad_piece)
    total_sq, loss_total = lax.psum((local_sq, loss_part), ("seq", "ffn"))
    grad_norm = jnp.sqrt(total_sq)
    clip_scale = jnp.minimum(1.0, CLIP_NORM / (grad_norm + 1e-06))
    weights = (attn_in, attn_out, ffn_in, ffn_out, tables, norm_params)
    firsts = (m_attn_in, m_attn_out, m_ffn_in, m_ffn_out, m_tables, m_norm_params)
    seconds = (v_attn_in, v_attn_out, v_ffn_in, v_ffn_out, v_tables, v_norm_params)
    results = [
        adam_step(
            weights[index],
            grad_list[index],
            firsts[index],
            seconds[index],
            STEP_RATES[index],
            clip_scale,
        )
        for index in range(6)
    ]
    return (
        results[0][0],
        results[1][0],
        results[2][0],
        results[3][0],
        results[4][0],
        results[5][0],
        results[0][1],
        results[1][1],
        results[2][1],
        results[3][1],
        results[4][1],
        results[5][1],
        results[0][2],
        results[1][2],
        results[2][2],
        results[3][2],
        results[4][2],
        results[5][2],
        grad_norm,
        loss_total,
    )


def solution(mesh):
    placed = (
        P("seq", None, "ffn"),
        P("ffn", "seq"),
        P("seq", "ffn"),
        P("ffn", "seq"),
        P(None, ("seq", "ffn")),
        P(None, ("seq", "ffn")),
        P("seq", None, "ffn"),
        P("ffn", "seq"),
        P("seq", "ffn"),
        P("ffn", "seq"),
        P(None, ("seq", "ffn")),
        P(None, ("seq", "ffn")),
        P("seq", None, "ffn"),
        P("ffn", "seq"),
        P("seq", "ffn"),
        P("ffn", "seq"),
        P(None, ("seq", "ffn")),
        P(None, ("seq", "ffn")),
        P(None, "seq"),
        P(None, ("seq", "ffn")),
        P(),
        P(),
        P(),
    )
    return jax.shard_map(
        per_device,
        mesh=mesh,
        in_specs=placed,
        out_specs=(
            P("seq", None, "ffn"),
            P("ffn", "seq"),
            P("seq", "ffn"),
            P("ffn", "seq"),
            P(None, ("seq", "ffn")),
            P(None, ("seq", "ffn")),
            P("seq", None, "ffn"),
            P("ffn", "seq"),
            P("seq", "ffn"),
            P("ffn", "seq"),
            P(None, ("seq", "ffn")),
            P(None, ("seq", "ffn")),
            P("seq", None, "ffn"),
            P("ffn", "seq"),
            P("seq", "ffn"),
            P("ffn", "seq"),
            P(None, ("seq", "ffn")),
            P(None, ("seq", "ffn")),
            P(),
            P(),
        ),
        check_vma=False,
    )
```

profile of v0, /device:TPU:0, one launch (start us, length us, event | category | flops | bytes accessed | tf_op | source)
XLA Modules:
  0.0 1481.8 jit_solution(1324214889330309181)
XLA Ops:
  13.9 70.4 %all-gather = bf16[32,32,6]{1,2,0:T(8,128)(2,1)S(1)} all-gather(bf16[1,32,6]{1,2,0:T(8,128)(2,1)S(1)} %convert_bitcast_fusion.2), channel_id=1, replica_groups=mesh['seq'=8,'ffn'=4] {'seq','ffn'}, dimensions={0}, use_global_device_ids=true | all-gather | bytes 12672 | tf_op jit(solution)/shard_map/all_gather | solution.py:168
  122.4 12.8 scatter_custom_fusion.3
  148.9 69.2 %reduce-window.16 = s32[2,2,8,32,4,128]{5,3,4,2,1,0:T(8,128)} reduce-window(s32[2,2,8,32,4,128]{5,3,4,2,1,0:T(8,128)} %compare_convert_fusion, s32[]{:T(128)} %constant.91.clone.1), window={size=1x1x1x1x1x128 pad=0_0x0_0x0_0x0_0x0_0x127_0}, to_apply=%region_5.6 | reduce-window | flops 66584576 | bytes 4194308 | tf_op jit(solution)/shard_map/reduce-window.2
  322.0 30.8 %all_gather.24 = bf16[256,1024]{1,0:T(8,128)(2,1)} all-gather(bf16[256,128]{1,0:T(8,128)(2,1)S(1)} %convert_element_type.238), channel_id=1, replica_groups=mesh['seq'=8,'ffn'=4] {'seq'}, dimensions={1}, use_global_device_ids=true | all-gather | bytes 589824 | tf_op jit(solution)/shard_map/all_gather | solution.py:162
  354.9 31.9 %gather_fusion.3 = f32[2048,2]{1,0:T(8,128)} fusion(f32[2,2,1024,2]{3,2,1,0:T(8,128)} %bitcast.306, s32[2048]{0:T(1024)S(1)} %bitcast.298), kind=kCustom, calls=%fused_computation.3 | custom fusion | bytes 57344 | tf_op jit(solution)/shard_map/jit(take_along_axis)/gather | solution.py:84
  396.3 35.1 %gather_fusion.4 = f32[2048,256]{1,0:T(8,128)} fusion(f32[2,2,1024,256]{3,2,1,0:T(8,128)} %bitcast.302, s32[2048]{0:T(1024)S(1)} %bitcast.299), kind=kCustom, calls=%fused_computation.4 | custom fusion | bytes 4218880 | tf_op jit(solution)/shard_map/jit(take_along_axis)/gather | solution.py:84
  452.4 79.6 %all-reduce.4.cloned.1.call-done = bf16[2,512,1024]{2,1,0:T(8,128)(2,1)} async-done(((bf16[2,512,1024]{2,1,0:T(8,128)(2,1)}), bf16[2,512,1024]{2,1,0:T(8,128)(2,1)}) %all-reduce.4.cloned.1.call-update) | async-done | bytes 2097168 | tf_op jit(solution)/shard_map/psum | solution.py:69
  543.4 17.8 %all-gather.11.cloned.1.call-done = bf16[1024,1024]{1,0:T(8,128)(2,1)} async-done(((bf16[128,1024]{1,0:T(8,128)(2,1)}), bf16[1024,1024]{1,0:T(8,128)(2,1)}) %all-gather.11.cloned.1.call-update) | async-done | bytes 2097168 | tf_op jit(solution)/shard_map/all_gather | solution.py:163
  568.9 22.7 %all-gather.13.cloned.1.call-done = bf16[1024,1024]{1,0:T(8,128)(2,1)} async-done(((bf16[1024,128]{1,0:T(8,128)(2,1)}), bf16[1024,1024]{1,0:T(8,128)(2,1)}) %all-gather.13.cloned.1.call-update) | async-done | bytes 2097168 | tf_op jit(solution)/shard_map/all_gather | solution.py:164
  599.0 42.3 %reduce-scatter.16.cloned.1.call-done = bf16[2,128,1024]{2,1,0:T(8,128)(2,1)} async-done(((bf16[2,512,1024]{2,1,0:T(8,128)(2,1)}), bf16[2,128,1024]{2,1,0:T(8,128)(2,1)}) %reduce-scatter.16.cloned.1.call-update) | async-done | bytes 524304 | tf_op jit(solution)/shard_map/reduce_scatter | solution.py:59
  647.1 44.8 %all-gather.15.cloned.1.call-done = bf16[2,512,1024]{2,1,0:T(8,128)(2,1)} async-done(((bf16[2,128,1024]{2,1,0:T(8,128)(2,1)}), bf16[2,512,1024]{2,1,0:T(8,128)(2,1)}) %all-gather.15.cloned.1.call-update) | async-done | bytes 2097168 | tf_op jit(solution)/shard_map/all_gather | solution.py:65
  712.2 77.1 %all-reduce.6.cloned.1.call-done = bf16[2,512,1024]{2,1,0:T(8,128)(2,1)} async-done(((bf16[2,512,1024]{2,1,0:T(8,128)(2,1)}), bf16[2,512,1024]{2,1,0:T(8,128)(2,1)}) %all-reduce.6.cloned.1.call-update) | async-done | bytes 2097168 | tf_op jit(solution)/shard_map/psum | solution.py:69
  824.9 14.0 scatter_custom_fusion.4
  864.0 59.5 %all-to-all-done.3 = bf16[2,2,8,128,768]{4,3,1,0,2:T(8,128)(2,1)} async-done(((bf16[2,2,8,128,768]{4,3,1,0,2:T(8,128)(2,1)}), bf16[2,2,8,128,768]{4,3,1,0,2:T(8,128)(2,1)}, u32[]{:S(2)}, u32[]{:S(2)}) %all-to-all-start.3) | async-done | bytes 6291488 | tf_op jit(solution)/shard_map/all_to_all | solution.py:316
  973.0 10.8 fusion.57
  990.0 16.5 %fusion.8 = bf16[2,2,32,32,2,128]{5,3,4,2,1,0:T(8,128)(2,1)} fusion(f32[2,2,32,32,2,128]{5,3,4,2,1,0:T(8,128)} %fusion, f32[2,2,32,2,128,32]{4,5,3,2,1,0:T(8,128)} %fusion.57, f32[2,2,32,32,2]{3,4,2,1,0:T(2,128)S(1)} %copy.521, f32[2,2,32,2,32,32]{4,5,3,2,1,0:T(8,128)} %copy-done.25, f32[2,2,32,2,32,32]{4,5,3,2,1,0:T(8,128)} %fusion.38, ...), kind=kOutput, calls=%fused_computation.30 | convolution fusion | flops 78913568 | bytes 14778368 | tf_op jit(solution)/shard_map/srbhij,srbjhc->srbihc/dot_general | solution.py:352
  1037.0 47.6 %all-to-all-done.5 = bf16[2,2,8,128,512]{4,3,1,0,2:T(8,128)(2,1)} async-done(((bf16[2,2,8,128,512]{4,3,1,0,2:T(8,128)(2,1)}), bf16[2,2,8,128,512]{4,3,1,0,2:T(8,128)(2,1)}, u32[]{:S(2)}, u32[]{:S(2)}) %all-to-all-start.5) | async-done | bytes 4194336 | tf_op jit(solution)/shard_map/all_to_all | solution.py:367
  1091.2 38.1 %gather_fusion.5 = f32[2048,512]{1,0:T(8,128)} fusion(f32[2,2,1024,512]{3,2,1,0:T(8,128)} %bitcast.301, s32[2048]{0:T(1024)S(1)} %bitcast.300), kind=kCustom, calls=%fused_computation.5 | custom fusion | bytes 8413184 | tf_op jit(solution)/shard_map/jit(take_along_axis)/gather | solution.py:84
  1133.3 8.6 fusion.10
  1172.8 10.8 scatter_custom_fusion
  1194.4 82.3 %reduce-scatter.28.cloned.1.call-done = f32[32,6]{1,0:T(8,128)} async-done(((f32[1024,6]{1,0:T(8,128)}), f32[32,6]{1,0:T(8,128)}) %reduce-scatter.28.cloned.1.call-update) | async-done | bytes 784
  1278.1 34.0 %reduce-scatter.18.cloned.1.call-done = bf16[128,2,256]{2,0,1:T(8,128)(2,1)} async-done(((bf16[1024,2,256]{2,0,1:T(8,128)(2,1)}), bf16[128,2,256]{2,0,1:T(8,128)(2,1)}) %reduce-scatter.18.cloned.1.call-update) | async-done | bytes 131088 | tf_op jit(solution)/shard_map/reduce_scatter | solution.py:396
  1316.3 103.3 %reduce-scatter.26.cloned.1.call-done = f32[32,672]{1,0:T(8,128)} async-done(((f32[1024,672]{1,0:T(8,128)}), f32[32,672]{1,0:T(8,128)}) %reduce-scatter.26.cloned.1.call-update) | async-done | bytes 86032
  1422.7 40.2 %all-reduce = (f32[]{:T(128)}, f32[]{:T(128)}) all-reduce(f32[]{:T(128)S(6)} %add.621, f32[]{:T(128)} %get-tuple-element.198), channel_id=1, replica_groups=mesh['seq'=8,'ffn'=4] {'seq','ffn'}, use_global_device_ids=true, to_apply=%region_64.65 | all-reduce | flops 2 | bytes 16 | tf_op jit(solution)/shard_map/psum | solution.py:413
  (416 shorter events, 460.3 us)
Async XLA Ops:
  7.2 81.6 %all-gather.7.cloned.1.call-start = ((), (), s32[]{:S(2)}) async-start(), calls=%async_computation.13 | async-start | bytes 1622016 | tf_op jit(solution)/shard_map/all_gather | solution.py:167
  8.8 104.4 %all-gather.9.cloned.1.call-start = ((), (), s32[]{:S(2)}) async-start(), calls=%async_computation.14 | async-start | bytes 1179648 | tf_op jit(solution)/shard_map/all_gather | solution.py:161
  139.7 101.0 %all-to-all-start = ((bf16[2,2,8,128,512]{4,3,1,0,2:T(8,128)(2,1)}), bf16[2,2,8,128,512]{4,3,1,0,2:T(8,128)(2,1)}, u32[]{:S(2)}, u32[]{:S(2)}) async-start(bf16[2,2,8,128,512]{4,3,1,0,2:T(8,128)(2,1)} %copy.475), calls=%async_computation | async-start | bytes 8388608 | tf_op jit(solution)/shard_map/all_to_all | solution.py:189
  294.2 22.5 %all-to-all-start.1 = ((bf16[2,2,8,128,2]{3,4,1,0,2:T(2,128)(2,1)}), bf16[2,2,8,128,2]{3,4,1,0,2:T(2,128)(2,1)S(1)}, u32[]{:S(2)}, u32[]{:S(2)}) async-start(bf16[2,2,8,128,2]{3,4,1,0,2:T(2,128)(2,1)} %copy.490), calls=%async_computation.1 | async-start | bytes 32768 | tf_op jit(solution)/shard_map/all_to_all | solution.py:234
  316.7 75.5 %all-to-all-start.2 = ((bf16[2,2,8,128,256]{4,3,1,0,2:T(8,128)(2,1)}), bf16[2,2,8,128,256]{4,3,1,0,2:T(8,128)(2,1)}, u32[]{:S(2)}, u32[]{:S(2)}) async-start(bf16[2,2,8,128,256]{4,3,1,0,2:T(8,128)(2,1)} %copy.499), calls=%async_computation.2 | async-start | bytes 4194304 | tf_op jit(solution)/shard_map/all_to_all | solution.py:227
  321.1 210.9 %all-reduce.4.cloned.1.call-start = ((), (), s32[]{:S(2)}) async-start(), calls=%async_computation.15 | async-start | bytes 4194304 | tf_op jit(solution)/shard_map/psum | solution.py:69
  448.5 112.6 %all-gather.11.cloned.1.call-start = ((), (), s32[]{:S(2)}) async-start(), calls=%async_computation.16 | async-start | bytes 2359296 | tf_op jit(solution)/shard_map/all_gather | solution.py:163
  450.4 141.2 %all-gather.13.cloned.1.call-start = ((), (), s32[]{:S(2)}) async-start(), calls=%async_computation.17 | async-start | bytes 2359296 | tf_op jit(solution)/shard_map/all_gather | solution.py:164
  452.3 189.0 %reduce-scatter.16.cloned.1.call-start = ((), (), s32[]{:S(2)}) async-start(), calls=%async_computation.18 | async-start | bytes 2621440 | tf_op jit(solution)/shard_map/reduce_scatter | solution.py:59
  597.5 94.4 %all-gather.15.cloned.1.call-start = ((), (), s32[]{:S(2)}) async-start(), calls=%async_computation.19 | async-start | bytes 2621440 | tf_op jit(solution)/shard_map/all_gather | solution.py:65
  646.9 142.4 %all-reduce.6.cloned.1.call-start = ((), (), s32[]{:S(2)}) async-start(), calls=%async_computation.20 | async-start | bytes 4194304 | tf_op jit(solution)/shard_map/psum | solution.py:69
  816.7 28.3 %all-to-all-start.4 = ((f32[2,2,8,128,2]{3,1,0,4,2:T(2,128)}), f32[2,2,8,128,2]{3,1,0,4,2:T(2,128)S(1)}, u32[]{:S(2)}, u32[]{:S(2)}) async-start(f32[2,2,8,128,2]{3,1,0,4,2:T(2,128)} %copy.515), calls=%async_computation.5 | async-start | bytes 65536 | tf_op jit(solution)/shard_map/all_to_all | solution.py:323
  845.0 78.6 %all-to-all-start.3 = ((bf16[2,2,8,128,768]{4,3,1,0,2:T(8,128)(2,1)}), bf16[2,2,8,128,768]{4,3,1,0,2:T(8,128)(2,1)}, u32[]{:S(2)}, u32[]{:S(2)}) async-start(bf16[2,2,8,128,768]{4,3,1,0,2:T(8,128)(2,1)} %copy.502), calls=%async_computation.4 | async-start | bytes 12582912 | tf_op jit(solution)/shard_map/all_to_all | solution.py:316
  849.9 339.2 %reduce-scatter.22.cloned.1.call-start = ((), (), s32[]{:S(2)}) async-start(), calls=%async_computation.23 | async-start | bytes 589824
  853.3 337.6 %reduce-scatter.24.cloned.1.call-start = ((), (), s32[]{:S(2)}) async-start(), calls=%async_computation.24 | async-start | bytes 2359296
  1025.2 59.5 %all-to-all-start.5 = ((bf16[2,2,8,128,512]{4,3,1,0,2:T(8,128)(2,1)}), bf16[2,2,8,128,512]{4,3,1,0,2:T(8,128)(2,1)}, u32[]{:S(2)}, u32[]{:S(2)}) async-start(bf16[2,2,8,128,512]{4,3,1,0,2:T(8,128)(2,1)} %copy.526), calls=%async_computation.6 | async-start | bytes 8388608 | tf_op jit(solution)/shard_map/all_to_all | solution.py:367
  1029.9 162.8 %reduce-scatter.20.cloned.1.call-start = ((), (), s32[]{:S(2)}) async-start(), calls=%async_computation.22 | async-start | bytes 2359296 | tf_op jit(solution)/shard_map/reduce_scatter | solution.py:402
  1036.9 239.8 %reduce-scatter.28.cloned.1.call-start = ((), (), s32[]{:S(2)}) async-start(), calls=%async_computation.26 | async-start | bytes 540672
  1143.0 169.1 %reduce-scatter.18.cloned.1.call-start = ((), (), s32[]{:S(2)}) async-start(), calls=%async_computation.21 | async-start | bytes 1179648 | tf_op jit(solution)/shard_map/reduce_scatter | solution.py:396
  1147.4 272.2 %reduce-scatter.26.cloned.1.call-start = ((), (), s32[]{:S(2)}) async-start(), calls=%async_computation.25 | async-start | bytes 3244032
  1189.1 279.3 %copy-start.36 = (f32[256,128]{1,0:T(8,128)S(1)}, f32[256,128]{1,0:T(8,128)}, u32[]{:S(2)}) copy-start(f32[256,128]{1,0:T(8,128)} %param.24) | copy-start | bytes 393220
  1190.2 279.9 %copy-start.28 = (f32[1024,128]{1,0:T(8,128)S(1)}, f32[1024,128]{1,0:T(8,128)}, u32[]{:S(2)}) copy-start(f32[1024,128]{1,0:T(8,128)} %param.26) | copy-start | bytes 1572868
  1190.2 279.9 %copy-start.37 = (f32[1024,128]{1,0:T(8,128)S(1)}, f32[1024,128]{1,0:T(8,128)}, u32[]{:S(2)}) copy-start(f32[1024,128]{1,0:T(8,128)} %param.32) | copy-start | bytes 1572868
  1190.2 279.9 %copy-start.38 = (f32[1024,128]{1,0:T(8,128)S(1)}, f32[1024,128]{1,0:T(8,128)}, u32[]{:S(2)}) copy-start(f32[1024,128]{1,0:T(8,128)} %param.38) | copy-start | bytes 1572868
  (75 other events, 1928.6 us)
Sparse Core Ops, SparseCore 0:
  11.4 57.7 all-gather.6
  71.7 22.4 all-gather.8
  448.6 83.2 all-reduce.3
  534.3 26.8 all-gather.10
  563.4 28.0 all-gather.12
  597.6 43.6 reduce-scatter.15
  647.0 44.8 all-gather.14
  704.3 84.9 all-reduce.5
  854.3 44.2 reduce-scatter.21
  901.8 48.1 reduce-scatter.23
  1037.1 51.7 reduce-scatter.19
  1143.1 133.5 reduce-scatter.27
  1279.9 32.1 reduce-scatter.17
  1317.4 102.1 reduce-scatter.25
where the time goes:
time: 1500 us; the launch traced here: 1480 us
  waiting for transfers between devices  611 us (41%)
  local copies, waits for them, and re-layouts  329 us (22%)
  other arithmetic  240 us (16%)
  blocking collectives  141 us (9%)
  matrix products  110 us (7%)
  starting transfers between devices  28 us (2%)
  between operations  21.5 us (1%)
    unnamed x18, waiting for transfers between devices  186 us
    psum x2, waiting for transfers between devices, total_rows(): return lax.psum(values.astype(jnp.bfloat16), 'ffn').astype(jnp.float32)  157 us
    gather x4, local copies, waits for them, and re-layouts, from_slots(): return jnp.take_along_axis(flat_rows, slot_index[..., None], axis=2)  108 us
    another operation x5, other arithmetic  71.3 us
    all_gather x1, blocking collectives, per_device(): lax.all_gather(norm_params.astype(jnp.bfloat16), ('seq', 'ffn'), axis=1,...  70.4 us
    all_to_all x1, waiting for transfers between devices, per_device(): lax.all_to_all(into_slots(send_rows, slot_index, total_slots, n_seq), 'se...  59.5 us
    unnamed x178, local copies, waits for them, and re-layouts  58.2 us
    all_to_all x1, waiting for transfers between devices, per_device(): lax.all_to_all(by_source(owner_grads, n_seq, CAP).astype(jnp.bfloat16), '...  47.6 us
  transfers between devices with their start and end apart: 20, of which 11 were waited for; matrix products, arithmetic and copies ran while one was open for 32% of the time, Pallas kernels for 0%

commit v1 on v0

v1 whole, which is shorter than its diff:
```python
import functools

import jax
import jax.numpy as jnp
from jax import lax
from jax.experimental import pallas as pl
from jax.experimental.pallas import tpu as pltpu
from jax.sharding import Mesh
from jax.sharding import PartitionSpec as P

HEAD = 128
VOCAB = 256
BUCKETS = 256
POS_LO = 128
STEP = 10


PENALTY = 10000.0
MASKED = -1000000000.0
LN_EPS = 1e-05
KEY_EPS = 1e-06
CLIP_NORM = 0.05
BETA_ONE = 0.9
BETA_TWO = 0.999
ADAM_EPS = 1e-08
WEIGHT_DECAY = 0.01
STEP_RATES = (0.1, 0.2, 0.1, 0.05, 0.5, 0.5)
LOG_TWO = 0.6931471805599453

CHIPS = ("pair", "sub")
SEQ = ("pair", "sub", "core")
ALL = ("pair", "sub", "core", "ffn")
F32 = jnp.float32
BF16 = jnp.bfloat16


def norm_forward(values, scale_row, shift_row):
    average = jnp.mean(values, axis=-1, keepdims=True)
    centred = values - average
    inv_std = lax.rsqrt(jnp.mean(centred * centred, axis=-1, keepdims=True) + LN_EPS)
    normal_part = centred * inv_std
    return (normal_part * scale_row + shift_row, normal_part, inv_std)


def norm_backward(upstream, normal_part, inv_std, scale_row):
    axes_list = tuple(range(upstream.ndim - 1))
    grad_scale = jnp.sum(upstream * normal_part, axis=axes_list)
    grad_shift = jnp.sum(upstream, axis=axes_list)
    scaled = upstream * scale_row
    grad_input = inv_std * (
        scaled
        - jnp.mean(scaled, axis=-1, keepdims=True)
        - normal_part * jnp.mean(scaled * normal_part, axis=-1, keepdims=True)
    )
    return (grad_input, grad_scale, grad_shift)


def adam_step(weight, grad_value, moment_one, moment_two, step_rate, clip_scale):
    clipped = grad_value * clip_scale
    new_one = BETA_ONE * moment_one + (1.0 - BETA_ONE) * clipped
    new_two = BETA_TWO * moment_two + (1.0 - BETA_TWO) * clipped * clipped
    fix_one = 1.0 - BETA_ONE**STEP
    fix_two = 1.0 - BETA_TWO**STEP
    change = new_one / fix_one / (jnp.sqrt(new_two / fix_two) + ADAM_EPS) + WEIGHT_DECAY * weight
    return (weight - step_rate * change, new_one, new_two)


def swap_core(values):
    return lax.ppermute(values, "core", [(0, 1), (1, 0)])


def spread_all(piece, axes):
    count = lax.axis_size(axes)
    copies = jnp.broadcast_to(piece[None], (count,) + piece.shape)
    own = lax.all_to_all(copies, axes, 0, 0, tiled=True)
    other = swap_core(own)
    first = lax.axis_index("core") == 0
    return jnp.where(first, jnp.stack([own, other], 1), jnp.stack([other, own], 1))


def sum_scatter(values, axes):
    core = lax.axis_index("core")
    keep = lax.dynamic_index_in_dim(values, core, 1, keepdims=False)
    give = lax.dynamic_index_in_dim(values, 1 - core, 1, keepdims=False)
    both = keep + swap_core(give.astype(BF16)).astype(F32)
    moved = lax.all_to_all(both.astype(BF16), axes, 0, 0, tiled=True)
    return jnp.sum(moved.astype(F32), axis=0)


def total_of(value):
    count = lax.axis_size(ALL)
    row = jnp.broadcast_to(value[None], (count,) + value.shape)
    return jnp.sum(lax.all_to_all(row, ALL, 0, 0, tiled=True), axis=0)


CONTRACT_LAST = (((1,), (1,)), ((), ()))
CONTRACT_FIRST = (((0,), (0,)), ((), ()))
PLAIN = (((1,), (0,)), ((), ()))


def mm(left, right, dims):
    return lax.dot_general(left, right, dims, preferred_element_type=F32)


def pair_counts(key_ids, query_ids, rounds):
    total = None
    for r in range(rounds):
        same = jnp.where(key_ids[:, r : r + 1] == query_ids[r : r + 1, :], 1.0, 0.0)
        total = same if total is None else total + same
    return total


def own_block(scores, counts, rounds):
    keys = lax.broadcasted_iota(jnp.int32, scores.shape, 0)
    queries = lax.broadcasted_iota(jnp.int32, scores.shape, 1)
    itself = keys == queries
    counts = jnp.where(itself, float(rounds), jnp.where(keys < queries, counts, 0.0))
    return jnp.where(itself, scores - PENALTY, scores), counts


def forward_kernel(
    rounds, info_ref, rows_ref, key_id_ref, query_id_ref, out_ref, wide_ref, stat_ref, unit_ref
):
    halves, pairs, seg = rows_ref.shape[:3]
    half = info_ref[0]

    def unit(step, carry):
        slot, pair = step // pairs, step % pairs
        rows = rows_ref[slot, pair, :, :HEAD].astype(F32)
        scale = lax.rsqrt(jnp.sum(rows * rows, axis=-1, keepdims=True) + KEY_EPS)
        unit_ref[slot, pair] = (rows * scale).astype(BF16)
        return carry

    lax.fori_loop(0, halves * pairs, unit, 0)

    def query_block(pair, carry):
        block = pair * halves + half
        own_slot = info_ref[1 + half]
        queries = rows_ref[own_slot, pair, :, :HEAD]
        query_ids = query_id_ref[block]

        def visit(index, state, diagonal):
            top, total, acc = state
            key_pair, slot = index // halves, info_ref[1 + index % halves]
            scores = mm(unit_ref[slot, key_pair], queries, CONTRACT_LAST)
            counts = pair_counts(key_id_ref[index], query_ids, rounds)
            if diagonal:
                scores, counts = own_block(scores, counts, rounds)
            new_top = jnp.maximum(
                top, jnp.max(jnp.where(counts > 0.0, scores, MASKED), axis=0, keepdims=True)
            )
            weights = jnp.where(counts > 0.0, jnp.exp(scores - new_top) * counts, 0.0)
            fade = jnp.exp(top - new_top)
            total = fade * total + jnp.sum(weights, axis=0, keepdims=True)
            values = rows_ref[slot, key_pair, :, HEAD:]
            acc = fade * acc + mm(values, weights.astype(BF16), CONTRACT_FIRST)
            return new_top, total, acc

        start = (
            jnp.full((1, seg), MASKED, F32),
            jnp.zeros((1, seg), F32),
            jnp.zeros((HEAD, seg), F32),
        )
        state = visit(block, start, True)
        top, total, acc = lax.fori_loop(
            0, block, lambda index, held: visit(index, held, False), state
        )
        inverse = 1.0 / total
        result = jnp.transpose(acc * inverse)
        out_ref[pair] = result.astype(BF16)
        wide_ref[pair] = result
        stat_ref[pair, 0:1, :] = top
        stat_ref[pair, 1:2, :] = inverse
        return carry

    lax.fori_loop(0, pairs, query_block, 0)


def backward_kernel(
    rounds,
    info_ref,
    rows_ref,
    key_id_ref,
    query_id_ref,
    unit_ref,
    grad_ref,
    wide_ref,
    stat_ref,
    query_grad_ref,
    key_grad_ref,
    value_grad_ref,
):
    halves, pairs, seg = rows_ref.shape[:3]
    half = info_ref[0]

    def clear(step, carry):
        zero = jnp.zeros((seg, HEAD), F32)
        key_grad_ref[step // pairs, step % pairs] = zero
        value_grad_ref[step // pairs, step % pairs] = zero
        return carry

    lax.fori_loop(0, halves * pairs, clear, 0)

    def query_block(pair, carry):
        block = pair * halves + half
        own_slot = info_ref[1 + half]
        queries = rows_ref[own_slot, pair, :, :HEAD]
        query_ids = query_id_ref[block]
        grads = grad_ref[pair]
        spent = grads.astype(F32) * wide_ref[pair]
        inner = jnp.sum(jnp.transpose(spent), axis=0, keepdims=True)
        top = stat_ref[pair, 0:1, :]
        inverse = stat_ref[pair, 1:2, :]

        def visit(index, acc, diagonal):
            key_pair, slot = index // halves, info_ref[1 + index % halves]
            keys = unit_ref[slot, key_pair]
            scores = mm(keys, queries, CONTRACT_LAST)
            counts = pair_counts(key_id_ref[index], query_ids, rounds)
            if diagonal:
                scores, counts = own_block(scores, counts, rounds)
            weights = jnp.where(counts > 0.0, jnp.exp(scores - top) * (counts * inverse), 0.0)
            value_grad_ref[slot, key_pair] += mm(weights.astype(BF16), grads, PLAIN)
            grad_weights = mm(rows_ref[slot, key_pair, :, HEAD:], grads, CONTRACT_LAST)
            grad_scores = (weights * (grad_weights - inner)).astype(BF16)
            key_grad_ref[slot, key_pair] += mm(grad_scores, queries, PLAIN)
            return acc + mm(keys, grad_scores, CONTRACT_FIRST)

        acc = visit(block, jnp.zeros((HEAD, seg), F32), True)
        acc = lax.fori_loop(0, block, lambda index, held: visit(index, held, False), acc)
        query_grad_ref[pair] = jnp.transpose(acc)
        return carry

    lax.fori_loop(0, pairs, query_block, 0)


def in_vmem(count):
    return [pl.BlockSpec(memory_space=pltpu.VMEM)] * count


def attend(info, rows, key_ids, query_ids, rounds):
    halves, pairs, seg = rows.shape[:3]
    return pl.pallas_call(
        functools.partial(forward_kernel, rounds),
        out_shape=(
            jax.ShapeDtypeStruct((pairs, seg, HEAD), BF16),
            jax.ShapeDtypeStruct((pairs, seg, HEAD), F32),
            jax.ShapeDtypeStruct((pairs, 2, seg), F32),
            jax.ShapeDtypeStruct((halves, pairs, seg, HEAD), BF16),
        ),
        in_specs=[pl.BlockSpec(memory_space=pltpu.SMEM)] + in_vmem(3),
        out_specs=tuple(in_vmem(4)),
        compiler_params=pltpu.CompilerParams(vmem_limit_bytes=56 << 20),
        name="attend",
    )(info, rows, key_ids, query_ids)


def attend_back(info, rows, key_ids, query_ids, unit, grads, wide, stats, rounds):
    halves, pairs, seg = rows.shape[:3]
    return pl.pallas_call(
        functools.partial(backward_kernel, rounds),
        out_shape=(
            jax.ShapeDtypeStruct((pairs, seg, HEAD), F32),
            jax.ShapeDtypeStruct((halves, pairs, seg, HEAD), F32),
            jax.ShapeDtypeStruct((halves, pairs, seg, HEAD), F32),
        ),
        in_specs=[pl.BlockSpec(memory_space=pltpu.SMEM)] + in_vmem(7),
        out_specs=tuple(in_vmem(3)),
        compiler_params=pltpu.CompilerParams(vmem_limit_bytes=56 << 20),
        name="attend_back",
    )(info, rows, key_ids, query_ids, unit, grads, wide, stats)


def per_device(
    attn_in,
    attn_out,
    ffn_in,
    ffn_out,
    tables,
    norm_params,
    m_attn_in,
    m_attn_out,
    m_ffn_in,
    m_ffn_out,
    m_tables,
    m_norm_params,
    v_attn_in,
    v_attn_out,
    v_ffn_in,
    v_ffn_out,
    v_tables,
    v_norm_params,
    tokens,
    targets,
    loss_mask,
    lengths,
    buckets,
):
    pairs, subs, cores, n_ffn = (lax.axis_size(axis) for axis in ALL)
    halves = subs * cores
    n_seq = pairs * halves
    chips = pairs * subs
    pair_rank = lax.axis_index("pair")
    half_rank = lax.axis_index("sub") * cores + lax.axis_index("core")
    seq_rank = pair_rank * halves + half_rank
    ffn_rank = lax.axis_index("ffn")
    num_seqs, seg_len = tokens.shape
    sub_len = targets.shape[1]
    full_len = loss_mask.shape[1]
    rounds = buckets.shape[1]
    upper_rows = full_len // POS_LO
    rows_total = tables.shape[0]
    slice_cols = tables.shape[1]
    width = slice_cols * n_seq * n_ffn
    head_width = attn_in.shape[2]
    heads_local = head_width // HEAD
    hid = ffn_in.shape[1]

    thin = jnp.concatenate([tables, norm_params], axis=0).astype(BF16).T
    thin_all = spread_all(thin, ("pair", "sub", "ffn"))
    thin_all = thin_all.reshape(chips, n_ffn, cores, slice_cols, thin.shape[1])
    thin_all = thin_all.transpose(0, 2, 1, 3, 4).reshape(width, thin.shape[1])
    table_all = thin_all[:, :rows_total]
    norm_rows = thin_all[:, rows_total:].T.astype(F32)
    w_in = spread_all(attn_in.astype(BF16).reshape(-1, 2 * head_width), CHIPS)
    w_in = w_in.reshape(width, 2 * head_width)
    w_out = lax.all_gather(attn_out.astype(BF16).T, ("ffn",) + SEQ, axis=0, tiled=True)
    w_out = w_out.reshape(n_ffn, width, head_width)
    w_up = lax.all_gather(ffn_in.astype(BF16), SEQ, axis=0, tiled=True)
    w_down = lax.all_gather(ffn_out.astype(BF16).T, SEQ, axis=0, tiled=True)

    seg_start = seq_rank * seg_len
    position = seg_start + jnp.arange(seg_len, dtype=jnp.int32)
    column = jnp.arange(rows_total, dtype=jnp.int32)
    hot = (
        (column == tokens[..., None])
        | (column == (2 * VOCAB + position // POS_LO)[None, :, None])
        | (column == (2 * VOCAB + upper_rows + position % POS_LO)[None, :, None])
    )
    hot = hot.astype(BF16).reshape(num_seqs * seg_len, rows_total)
    embedded = mm(hot, table_all, CONTRACT_LAST)
    normed_full, normal_one, inv_one = norm_forward(embedded, norm_rows[0], norm_rows[1])
    normed = normed_full.astype(BF16)

    def own_rows(values):
        whole = values.reshape(num_seqs, seg_len, -1)
        return lax.dynamic_slice_in_dim(whole, ffn_rank * sub_len, sub_len, 1).reshape(
            num_seqs * sub_len, -1
        )

    own_embed = own_rows(embedded)

    projected = mm(normed, w_in, PLAIN).astype(BF16)
    projected = projected.reshape(num_seqs, seg_len, 2, heads_local, HEAD)
    projected = projected.transpose(0, 3, 1, 2, 4).reshape(pairs, seg_len, 2 * HEAD)
    own = lax.all_to_all(projected, "pair", 0, 0, tiled=True)
    if subs == 1:
        rows = jnp.stack([own, swap_core(own)])
        slots = jnp.arange(halves, dtype=jnp.int32) ^ half_rank
    else:
        rows = lax.all_gather(own, ("sub", "core"), axis=0, tiled=False)
        slots = jnp.arange(halves, dtype=jnp.int32)
    info = jnp.concatenate([half_rank[None].astype(jnp.int32), slots.astype(jnp.int32)])
    my_seq = pair_rank // heads_local
    my_ids = lax.dynamic_index_in_dim(buckets[..., 0], my_seq, 0, keepdims=False)
    my_length = lax.dynamic_index_in_dim(lengths, my_seq, 0, keepdims=False)
    query_ids = my_ids.reshape(rounds, n_seq, seg_len).transpose(1, 0, 2)
    usable = jnp.arange(full_len, dtype=jnp.int32) < my_length
    key_ids = jnp.where(usable[:, None], my_ids.T, -1).reshape(n_seq, seg_len, rounds)
    out, wide, stats, unit = attend(info, rows, key_ids, query_ids, rounds)

    both = ("pair", "ffn")
    moved = lax.all_to_all(
        out.reshape(pairs * n_ffn, sub_len, HEAD), both, 0, 0, tiled=True
    )
    moved = moved.reshape(num_seqs, heads_local, n_ffn, sub_len, HEAD)
    attended = moved.transpose(0, 3, 2, 1, 4).reshape(num_seqs * sub_len, n_ffn, head_width)
    branch = jnp.einsum("rzc,zdc->rd", attended, w_out, preferred_element_type=F32)

    def whole_rows(values):
        split = values.reshape(num_seqs, sub_len, -1)
        return lax.all_gather(split, "ffn", axis=1, tiled=True).reshape(num_seqs * seg_len, -1)

    def share_rows(values):
        split = values.astype(BF16).reshape(num_seqs, seg_len, -1)
        return (
            lax.psum_scatter(split, "ffn", scatter_dimension=1, tiled=True)
            .reshape(num_seqs * sub_len, -1)
            .astype(F32)
        )

    first_out = own_embed + branch
    middle_own, normal_two, inv_two = norm_forward(first_out, norm_rows[2], norm_rows[3])
    middle = whole_rows(middle_own.astype(BF16))
    pre_act = mm(middle, w_up, PLAIN)
    hidden = jnp.maximum(pre_act, 0.0).astype(BF16)
    second_out = own_embed + share_rows(mm(hidden, w_down, CONTRACT_LAST))
    final_full, normal_three, inv_three = norm_forward(
        first_out + second_out, norm_rows[4], norm_rows[5]
    )
    final_rows = final_full.astype(BF16)

    head_cols = table_all[:, VOCAB : 2 * VOCAB]
    logits = mm(final_rows, head_cols, PLAIN)
    log_norm = jax.nn.logsumexp(logits, axis=-1)
    wanted = targets.reshape(num_seqs * sub_len)
    target_hot = (wanted[:, None] == jnp.arange(VOCAB, dtype=jnp.int32)).astype(F32)
    picked = jnp.sum(logits * target_hot, axis=-1)
    bits_lost = (log_norm - picked) / LOG_TWO
    live_all = (
        loss_mask * (jnp.arange(full_len, dtype=jnp.int32)[None, :] < lengths[:, None])
    ).astype(F32)
    counts = jnp.sum(live_all, axis=1)
    live_own = lax.dynamic_slice_in_dim(live_all, seg_start + ffn_rank * sub_len, sub_len, 1)
    weight_row = lengths.astype(F32) / full_len / counts
    loss_weight = (live_own * weight_row[:, None]).reshape(num_seqs * sub_len)
    loss_part = jnp.sum(loss_weight * bits_lost)
    softmax_p = jnp.exp(logits - log_norm[:, None])
    grad_logits = ((loss_weight / LOG_TWO)[:, None] * (softmax_p - target_hot)).astype(BF16)
    grad_final = mm(grad_logits, head_cols, CONTRACT_LAST)
    grad_head = mm(final_rows, grad_logits, CONTRACT_FIRST)
    grad_sum, gain_five, bias_five = norm_backward(
        grad_final, normal_three, inv_three, norm_rows[4]
    )

    rows_grad = whole_rows(grad_sum.astype(BF16))
    grad_hidden = mm(rows_grad, w_down, PLAIN)
    grad_pre = jnp.where(pre_act > 0.0, grad_hidden, 0.0).astype(BF16)
    grad_middle = share_rows(mm(grad_pre, w_up, CONTRACT_LAST))
    grad_down = mm(rows_grad, hidden, CONTRACT_FIRST)
    grad_up = mm(middle, grad_pre, CONTRACT_FIRST)
    first_part, gain_three, bias_three = norm_backward(
        grad_middle, normal_two, inv_two, norm_rows[2]
    )
    grad_first = first_part + grad_sum

    grad_branch = grad_first.astype(BF16)
    grad_out = jnp.einsum("rzc,rd->zdc", attended, grad_branch, preferred_element_type=F32)
    grad_att = jnp.einsum("rd,zdc->rzc", grad_branch, w_out, preferred_element_type=F32)
    grad_att = grad_att.astype(BF16).reshape(num_seqs, sub_len, n_ffn, heads_local, HEAD)
    grad_att = grad_att.transpose(0, 3, 2, 1, 4).reshape(pairs * n_ffn, sub_len, HEAD)
    grads = lax.all_to_all(grad_att, both, 0, 0, tiled=True).reshape(pairs, seg_len, HEAD)
    query_grad, key_grad, value_grad = attend_back(
        info, rows, key_ids, query_ids, unit, grads, wide, stats, rounds
    )
    if subs == 1:
        away = jnp.concatenate([key_grad[1], value_grad[1]], axis=-1).astype(BF16)
        came = swap_core(away).astype(F32)
        keys_total = key_grad[0] + came[..., :HEAD]
        values_total = value_grad[0] + came[..., HEAD:]
    else:
        away = jnp.concatenate([key_grad, value_grad], axis=-1).astype(BF16)
        came = lax.psum_scatter(away, ("sub", "core"), scatter_dimension=0).astype(F32)
        keys_total, values_total = came[..., :HEAD], came[..., HEAD:]
    widened = own[..., :HEAD].astype(F32)
    inv_norm = lax.rsqrt(jnp.sum(widened * widened, axis=-1, keepdims=True) + KEY_EPS)
    grad_qk = (
        query_grad
        + keys_total * inv_norm
        - widened * inv_norm**3 * jnp.sum(widened * keys_total, axis=-1, keepdims=True)
    )
    owner_grads = jnp.concatenate([grad_qk, values_total], axis=-1).astype(BF16)
    grad_proj = lax.all_to_all(owner_grads, "pair", 0, 0, tiled=True)
    grad_proj = grad_proj.reshape(num_seqs, heads_local, seg_len, 2, HEAD)
    grad_proj = grad_proj.transpose(0, 2, 3, 1, 4).reshape(num_seqs * seg_len, 2 * head_width)
    grad_in = mm(normed, grad_proj, CONTRACT_FIRST)
    grad_normed = mm(grad_proj, w_in, CONTRACT_LAST)
    embed_part, gain_one, bias_one = norm_backward(grad_normed, normal_one, inv_one, norm_rows[0])
    whole = embed_part.reshape(num_seqs, seg_len, width)
    extra = (grad_first + grad_sum).reshape(num_seqs, sub_len, width)
    own_total = lax.dynamic_slice_in_dim(whole, ffn_rank * sub_len, sub_len, 1) + extra
    whole = lax.dynamic_update_slice_in_dim(whole, own_total, ffn_rank * sub_len, 1)
    embed_grad = whole.reshape(num_seqs * seg_len, width).astype(BF16)
    grad_tables = mm(embed_grad, hot, CONTRACT_FIRST)
    grad_tables = grad_tables + jnp.pad(
        grad_head, ((0, 0), (VOCAB, rows_total - 2 * VOCAB))
    )
    grad_norms = jnp.stack(
        [gain_one, bias_one, gain_three, bias_three, gain_five, bias_five], axis=1
    )

    thin_grad = jnp.concatenate([grad_tables, grad_norms], axis=1)
    thin_grad = thin_grad.reshape(chips, cores, n_ffn, slice_cols, -1).transpose(0, 2, 1, 3, 4)
    thin_grad = sum_scatter(
        thin_grad.reshape(chips * n_ffn, cores, slice_cols, -1), ("pair", "sub", "ffn")
    ).T
    table_grad, norm_grad = thin_grad[:rows_total], thin_grad[rows_total:]
    in_grad = sum_scatter(grad_in.reshape(chips, cores, -1, 2 * head_width), CHIPS)
    in_grad = in_grad.reshape(attn_in.shape)
    out_grad = lax.psum_scatter(
        grad_out.astype(BF16).reshape(n_ffn * width, head_width),
        ("ffn",) + SEQ,
        scatter_dimension=0,
        tiled=True,
    )
    out_grad = out_grad.astype(F32).T
    up_grad = sum_scatter(grad_up.reshape(chips, cores, -1, hid), CHIPS)
    down_grad = sum_scatter(grad_down.reshape(chips, cores, -1, hid), CHIPS).T

    grad_list = (in_grad, out_grad, up_grad, down_grad, table_grad, norm_grad)
    local_sq = jnp.float32(0.0)
    for grad_piece in grad_list:
        local_sq = local_sq + jnp.sum(grad_piece * grad_piece)
    totals = total_of(jnp.stack([local_sq, loss_part]))
    total_sq, loss_total = totals[0], totals[1]
    grad_norm = jnp.sqrt(total_sq)
    clip_scale = jnp.minimum(1.0, CLIP_NORM / (grad_norm + 1e-06))
    weights = (attn_in, attn_out, ffn_in, ffn_out, tables, norm_params)
    firsts = (m_attn_in, m_attn_out, m_ffn_in, m_ffn_out, m_tables, m_norm_params)
    seconds = (v_attn_in, v_attn_out, v_ffn_in, v_ffn_out, v_tables, v_norm_params)
    results = [
        adam_step(
            weights[index],
            grad_list[index],
            firsts[index],
            seconds[index],
            STEP_RATES[index],
            clip_scale,
        )
        for index in range(6)
    ]
    return tuple(results[index][part] for part in range(3) for index in range(6)) + (
        grad_norm,
        loss_total,
    )


def solution(mesh):
    n_seq, n_ffn = mesh.shape["seq"], mesh.shape["ffn"]

    def step(*args):
        num_pairs = args[18].shape[0] * (args[0].shape[2] // HEAD // n_ffn)
        subs = n_seq // 2 // num_pairs
        fine = Mesh(mesh.devices.reshape(num_pairs, subs, 2, n_ffn), ALL)
        weights = (
            P(SEQ, None, "ffn"),
            P("ffn", SEQ),
            P(SEQ, "ffn"),
            P("ffn", SEQ),
            P(None, ALL),
            P(None, ALL),
        )
        return jax.shard_map(
            per_device,
            mesh=fine,
            in_specs=weights * 3 + (P(None, SEQ), P(None, ALL), P(), P(), P()),
            out_specs=weights * 3 + (P(), P()),
            check_vma=False,
        )(*args)

    return step
```

time: 1500 us -> 663 us (0.44)
  waiting for transfers between devices: 611 us -> 316 us
  local copies, waits for them, and re-layouts: 329 us -> 91 us
  other arithmetic: 240 us -> 70.7 us
  blocking collectives: 141 us -> 0 us
  matrix products: 110 us -> 57.3 us
  Pallas kernels: 0 us -> 42.4 us
  starting transfers between devices: 28 us -> 53 us
    psum x2 -> x0, waiting for transfers between devices: 157 us -> none  [total_rows(): return lax.psum(values.astype(jnp.bfloat16), 'ffn').astype(jnp.float32)]
    unnamed x18 -> x9, waiting for transfers between devices: 186 us -> 63.4 us
    gather x7 -> x0, local copies, waits for them, and re-layouts: 119 us -> none  [the longest x4 108 us: from_slots(): return jnp.take_along_axis(flat_rows, slot_index[..., None], axis=2)]
    all_gather x2 -> x0, blocking collectives: 101 us -> none  [the longest x1 70.4 us: per_device(): lax.all_gather(norm_params.astype(jnp.bfloat16), ('seq', 'ffn'), axis=1,...]
    another operation x5, other arithmetic: 71.3 us -> 2.37 us  [the longest x1 1.48 us: per_device(): rows = jnp.stack([own, swap_core(own)])]
    dot_general x22 -> x17, matrix products: 110 us -> 57.3 us  [the longest x14 51.9 us: mm(): return lax.dot_general(left, right, dims, preferred_element_type=F32)]
    pallas_call x0 -> x2, Pallas kernels: none -> 42.4 us  [the longest x1 22.5 us: attend_back(): pl.pallas_call(functools.partial(backward_kernel, rounds), out_shape=(jax...]
    psum x1 -> x0, blocking collectives: 40.2 us -> none  [per_device(): total_sq, loss_total = lax.psum((local_sq, loss_part), ('seq', 'ffn'))]
  transfers between devices with their start and end apart: 20 -> 27, of which waited for: 11 -> 15; matrix products, arithmetic and copies ran while one was open for 32% -> 23% of each run, Pallas kernels for 0% -> 3%
where the time goes in v1:
time: 663 us; the launch traced here: 652 us
  waiting for transfers between devices  316 us (48%)
  local copies, waits for them, and re-layouts  91 us (14%)
  other arithmetic  70.7 us (11%)
  matrix products  57.3 us (9%)
  starting transfers between devices  53 us (8%)
  Pallas kernels  42.4 us (6%)
  between operations  21.5 us (3%)
    all_gather x2, waiting for transfers between devices, whole_rows(): lax.all_gather(split, 'ffn', axis=1, tiled=True)  87.1 us
    reduce_scatter x2, waiting for transfers between devices, share_rows(): lax.psum_scatter(split, 'ffn', scatter_dimension=1, tiled=True)  74.6 us
    unnamed x9, waiting for transfers between devices  63.4 us
    dot_general x14, matrix products, mm(): return lax.dot_general(left, right, dims, preferred_element_type=F32)  51.9 us
    all_to_all x2, waiting for transfers between devices, spread_all(): own = lax.all_to_all(copies, axes, 0, 0, tiled=True)  27.7 us
    unnamed x171, local copies, waits for them, and re-layouts  25.6 us
    all_gather x1, waiting for transfers between devices, per_device(): w_down = lax.all_gather(ffn_out.astype(BF16).T, SEQ, axis=0, tiled=True)  22.7 us
    pallas_call x1, Pallas kernels, attend_back(): pl.pallas_call(functools.partial(backward_kernel, rounds), out_shape=(jax...  22.5 us
  transfers between devices with their start and end apart: 27, of which 15 were waited for; matrix products, arithmetic and copies ran while one was open for 23% of the time, Pallas kernels for 3%

profile of v1, /device:TPU:0, one launch (start us, length us, event | category | flops | bytes accessed | tf_op | source)
XLA Modules:
  0.0 652.1 jit_solution(18201107731324806566)
XLA Ops:
  9.2 5.3 all-to-all-start.1
  14.7 7.8 %all-to-all-done.1 = bf16[4,128,512]{2,1,0:T(8,128)(2,1)S(1)} async-done(((bf16[4,128,512]{2,1,0:T(8,128)(2,1)}), bf16[4,128,512]{2,1,0:T(8,128)(2,1)S(1)}, u32[]{:S(2)}, u32[]{:S(2)}) %all-to-all-start.1) | async-done | bytes 524320 | tf_op jit(solution)/shard_map/all_to_all | solution.py:75
  23.5 5.9 all-to-all-start
  30.2 19.9 %all-to-all-done = bf16[16,32,678]{2,1,0:T(8,128)(2,1)S(1)} async-done(((bf16[16,32,678]{2,1,0:T(8,128)(2,1)}), bf16[16,32,678]{2,1,0:T(8,128)(2,1)S(1)}, u32[]{:S(2)}, u32[]{:S(2)}) %all-to-all-start) | async-done | bytes 694304 | tf_op jit(solution)/shard_map/all_to_all | solution.py:75
  73.7 16.9 %all-to-all-done.2 = bf16[4,512,256]{2,1,0:T(8,128)(2,1)S(1)} async-done(((bf16[4,512,256]{2,1,0:T(8,128)(2,1)}), bf16[4,512,256]{2,1,0:T(8,128)(2,1)S(1)}, u32[]{:S(2)}, u32[]{:S(2)}) %all-to-all-start.2) | async-done | bytes 1048608 | tf_op jit(solution)/shard_map/all_to_all | solution.py:356
  94.9 19.9 %attend.1 = (bf16[4,512,128]{2,1,0:T(8,128)(2,1)}, f32[4,512,128]{2,1,0:T(8,128)}, f32[4,2,512]{2,1,0:T(2,128)}, bf16[2,4,512,128]{3,2,1,0:T(8,128)(2,1)}) custom-call(s32[3]{0:T(128)} %pad_add_fusion.info_ref, bf16[2,4,512,256]{3,2,1,0:T(8,128)(2,1)} %pad_maximum_fusion.rows_ref, s32[8,512,2]{2,1,0:T(8,128)} %bitcast.230, s32[8,2,512]{2,1,0:T(2,128)} %bitcast.278), custom_call_target="tpu_custom_call" | custom-call | tf_op jit(solution)/shard_map/attend/pallas_call | solution.py:243
  124.3 10.6 %all-to-all-done.3 = bf16[16,128,128]{2,1,0:T(8,128)(2,1)S(1)} async-done(((bf16[16,128,128]{2,1,0:T(8,128)(2,1)}), bf16[16,128,128]{2,1,0:T(8,128)(2,1)S(1)}, u32[]{:S(2)}, u32[]{:S(2)}) %all-to-all-start.3) | async-done | bytes 524320 | tf_op jit(solution)/shard_map/all_to_all | solution.py:373
  142.7 42.1 %all-gather.8.cloned.1.call-done = bf16[2,512,1024]{2,1,0:T(8,128)(2,1)} async-done(((bf16[2,128,1024]{2,1,0:T(8,128)(2,1)}), bf16[2,512,1024]{2,1,0:T(8,128)(2,1)}) %all-gather.8.cloned.1.call-update) | async-done | bytes 2097168 | tf_op jit(solution)/shard_map/all_gather | solution.py:382
  184.8 6.5 %fusion.106 = f32[1024,1024]{1,0:T(8,128)} fusion(bf16[1024,1024]{1,0:T(8,128)(2,1)} %bitcast.255, bf16[1024,1024]{1,0:T(8,128)(2,1)} %all-gather.10.cloned.1.call-done), kind=kOutput, calls=%fused_computation.228 | convolution fusion | flops 2147483648 | bytes 8388608 | tf_op jit(solution)/shard_map/dot_general | solution.py:102
  191.3 22.7 %all-gather.12.cloned.1.call-done = bf16[1024,1024]{0,1:T(8,128)(2,1)} async-done(((bf16[128,1024]{0,1:T(8,128)(2,1)}), bf16[1024,1024]{0,1:T(8,128)(2,1)}) %all-gather.12.cloned.1.call-update) | async-done | bytes 2097168 | tf_op jit(solution)/shard_map/all_gather | solution.py:330
  214.0 6.5 %convolution_convert_fusion.2 = bf16[1024,1024]{1,0:T(8,128)(2,1)} fusion(bf16[1024,1024]{0,1:T(8,128)(2,1)} %all-gather.12.cloned.1.call-done, f32[1024,1024]{1,0:T(8,128)} %fusion.106), kind=kOutput, calls=%fused_computation.35 | convolution fusion | flops 2150629376 | bytes 8388608 | tf_op jit(solution)/shard_map/dot_general | solution.py:102
  223.4 41.0 %reduce-scatter.6.cloned.1.call-done = bf16[2,128,1024]{2,1,0:T(8,128)(2,1)} async-done(((bf16[2,512,1024]{2,1,0:T(8,128)(2,1)}), bf16[2,128,1024]{2,1,0:T(8,128)(2,1)}) %reduce-scatter.6.cloned.1.call-update) | async-done | bytes 524304 | tf_op jit(solution)/shard_map/reduce_scatter | solution.py:387
  271.8 45.0 %all-gather.14.cloned.1.call-done = bf16[2,512,1024]{2,1,0:T(8,128)(2,1)} async-done(((bf16[2,128,1024]{2,1,0:T(8,128)(2,1)}), bf16[2,512,1024]{2,1,0:T(8,128)(2,1)}) %all-gather.14.cloned.1.call-update) | async-done | bytes 2097168 | tf_op jit(solution)/shard_map/all_gather | solution.py:382
  316.7 6.0 select_convert_fusion
  335.5 33.6 %reduce-scatter.8.cloned.1.call-done = bf16[2,128,1024]{2,1,0:T(8,128)(2,1)} async-done(((bf16[2,512,1024]{2,1,0:T(8,128)(2,1)}), bf16[2,128,1024]{2,1,0:T(8,128)(2,1)}) %reduce-scatter.8.cloned.1.call-update) | async-done | bytes 524304 | tf_op jit(solution)/shard_map/reduce_scatter | solution.py:387
  377.2 5.0 all-to-all-start.4
  391.1 7.1 %fusion.9 = f32[4,2,128,1024]{3,2,1,0:T(8,128)} fusion(bf16[4,2,128,1024]{3,2,1,0:T(8,128)(2,1)} %bitcast.263, f32[1024,1024]{1,0:T(8,128)} %fusion.106), kind=kOutput, calls=%fused_computation.20 | convolution fusion | flops 2149580800 | bytes 10485760 | tf_op jit(solution)/shard_map/dot_general | solution.py:102
  399.1 22.5 %attend_back.1 = (f32[4,512,128]{2,1,0:T(8,128)}, f32[2,4,512,128]{3,2,1,0:T(8,128)}, f32[2,4,512,128]{3,2,1,0:T(8,128)}) custom-call(s32[3]{0:T(128)} %pad_add_fusion.info_ref, bf16[2,4,512,256]{3,2,1,0:T(8,128)(2,1)} %pad_maximum_fusion.rows_ref, s32[8,512,2]{2,1,0:T(8,128)} %bitcast.231, s32[8,2,512]{2,1,0:T(2,128)} %bitcast.279, ...), custom_call_target="tpu_custom_call" | custom-call | tf_op jit(solution)/shard_map/attend_back/pallas_call | solution.py:260
  477.1 5.5 multiply_reduce_fusion
  494.7 5.5 bitcast_add_fusion
  504.9 5.7 concatenate.46
  522.4 8.4 %all-to-all-done.6 = bf16[4,128,512]{2,1,0:T(8,128)(2,1)} async-done(((bf16[4,128,512]{2,1,0:T(8,128)(2,1)}), bf16[4,128,512]{2,1,0:T(8,128)(2,1)}, u32[]{:S(2)}, u32[]{:S(2)}) %all-to-all-start.6) | async-done | bytes 524320 | tf_op jit(solution)/shard_map/all_to_all | solution.py:86
  530.8 5.6 all-to-all-start.9
  541.5 63.2 %reduce-scatter.10.cloned.1.call-done = bf16[128,256]{1,0:T(8,128)(2,1)} async-done(((bf16[4096,256]{1,0:T(8,128)(2,1)}), bf16[128,256]{1,0:T(8,128)(2,1)}) %reduce-scatter.10.cloned.1.call-update) | async-done | bytes 65552
  (351 shorter events, 212.2 us)
Async XLA Ops:
  9.2 13.3 %all-to-all-start.1 = ((bf16[4,128,512]{2,1,0:T(8,128)(2,1)}), bf16[4,128,512]{2,1,0:T(8,128)(2,1)S(1)}, u32[]{:S(2)}, u32[]{:S(2)}) async-start(bf16[4,128,512]{2,1,0:T(8,128)(2,1)} %broadcast_in_dim.30), calls=%async_computation.1 | async-start | bytes 1048576 | tf_op jit(solution)/shard_map/all_to_all | solution.py:75
  23.5 26.6 %all-to-all-start = ((bf16[16,32,678]{2,1,0:T(8,128)(2,1)}), bf16[16,32,678]{2,1,0:T(8,128)(2,1)S(1)}, u32[]{:S(2)}, u32[]{:S(2)}) async-start(bf16[16,32,678]{2,1,0:T(8,128)(2,1)} %broadcast_in_dim.27), calls=%async_computation | async-start | bytes 1572864 | tf_op jit(solution)/shard_map/all_to_all | solution.py:75
  29.4 90.8 %all-gather.6.cloned.1.call-start = ((), (), s32[]{:S(2)}) async-start(), calls=%async_computation.14 | async-start | bytes 2162688 | tf_op jit(solution)/shard_map/all_gather | solution.py:327
  30.1 20.6 %collective-permute-start.1 = (bf16[4,128,512]{2,1,0:T(8,128)(2,1)S(1)}, bf16[4,128,512]{2,1,0:T(8,128)(2,1)S(1)}, u32[]{:S(2)}, u32[]{:S(2)}) collective-permute-start(bf16[4,128,512]{2,1,0:T(8,128)(2,1)S(1)} %all-to-all-done.1), channel_id=1, source_target_pairs={{0,4},{4,0},{1,5},{5,1},{2,6},{6,2},{3,7},{7,3},{8,12},{12,8},{9,1... | collective-permute-start | bytes 1572872 | tf_op jit(solution)/shard_map/ppermute | solution.py:69
  67.2 23.4 %all-to-all-start.2 = ((bf16[4,512,256]{2,1,0:T(8,128)(2,1)}), bf16[4,512,256]{2,1,0:T(8,128)(2,1)S(1)}, u32[]{:S(2)}, u32[]{:S(2)}) async-start(bf16[4,512,256]{2,1,0:T(8,128)(2,1)} %reshape.393), calls=%async_computation.2 | async-start | bytes 2097152 | tf_op jit(solution)/shard_map/all_to_all | solution.py:356
  70.9 71.8 %all-gather.10.cloned.1.call-start = ((), (), s32[]{:S(2)}) async-start(), calls=%async_computation.16 | async-start | bytes 2359296 | tf_op jit(solution)/shard_map/all_gather | solution.py:329
  114.8 20.0 %all-to-all-start.3 = ((bf16[16,128,128]{2,1,0:T(8,128)(2,1)}), bf16[16,128,128]{2,1,0:T(8,128)(2,1)S(1)}, u32[]{:S(2)}, u32[]{:S(2)}) async-start(bf16[16,128,128]{2,1,0:T(8,128)(2,1)} %bitcast.277), calls=%async_computation.3 | async-start | bytes 1048576 | tf_op jit(solution)/shard_map/all_to_all | solution.py:373
  118.8 66.0 %all-gather.8.cloned.1.call-start = ((), (), s32[]{:S(2)}) async-start(), calls=%async_computation.15 | async-start | bytes 2621440 | tf_op jit(solution)/shard_map/all_gather | solution.py:382
  140.8 73.3 %all-gather.12.cloned.1.call-start = ((), (), s32[]{:S(2)}) async-start(), calls=%async_computation.17 | async-start | bytes 2359296 | tf_op jit(solution)/shard_map/all_gather | solution.py:330
  142.6 121.8 %reduce-scatter.6.cloned.1.call-start = ((), (), s32[]{:S(2)}) async-start(), calls=%async_computation.18 | async-start | bytes 2621440 | tf_op jit(solution)/shard_map/reduce_scatter | solution.py:387
  220.6 96.1 %all-gather.14.cloned.1.call-start = ((), (), s32[]{:S(2)}) async-start(), calls=%async_computation.19 | async-start | bytes 2621440 | tf_op jit(solution)/shard_map/all_gather | solution.py:382
  271.7 97.4 %reduce-scatter.8.cloned.1.call-start = ((), (), s32[]{:S(2)}) async-start(), calls=%async_computation.20 | async-start | bytes 2621440 | tf_op jit(solution)/shard_map/reduce_scatter | solution.py:387
  377.2 21.1 %all-to-all-start.4 = ((bf16[16,128,128]{2,1,0:T(8,128)(2,1)}), bf16[16,128,128]{2,1,0:T(8,128)(2,1)S(1)}, u32[]{:S(2)}, u32[]{:S(2)}) async-start(bf16[16,128,128]{2,1,0:T(8,128)(2,1)} %bitcast.44), calls=%async_computation.6 | async-start | bytes 1048576 | tf_op jit(solution)/shard_map/all_to_all | solution.py:442
  425.3 15.2 %collective-permute-start.3 = (bf16[4,512,256]{2,1,0:T(8,128)(2,1)}, bf16[4,512,256]{2,1,0:T(8,128)(2,1)}, u32[]{:S(2)}, u32[]{:S(2)}) collective-permute-start(bf16[4,512,256]{2,1,0:T(8,128)(2,1)} %pad_maximum_fusion.1), channel_id=1, source_target_pairs={{0,4},{4,0},{1,5},{5,1},{2,6},{6,2},{3,7},{7,3},{8,12},{12,8},{9,1... | collective-permute-start | bytes 3145736 | tf_op jit(solution)/shard_map/ppermute | solution.py:69
  431.8 20.8 %collective-permute-start.6 = (bf16[4,128,1024]{2,1,0:T(8,128)(2,1)}, bf16[4,128,1024]{2,1,0:T(8,128)(2,1)}, u32[]{:S(2)}, u32[]{:S(2)}) collective-permute-start(bf16[4,128,1024]{2,1,0:T(8,128)(2,1)} %fusion.30), channel_id=1, source_target_pairs={{0,4},{4,0},{1,5},{5,1},{2,6},{6,2},{3,7},{7,3},{8,12},{12,8},{9,1... | collective-permute-start | bytes 3145736 | tf_op jit(solution)/shard_map/ppermute | solution.py:69
  436.0 20.0 %collective-permute-start.5 = (bf16[4,128,1024]{2,1,0:T(8,128)(2,1)}, bf16[4,128,1024]{2,1,0:T(8,128)(2,1)}, u32[]{:S(2)}, u32[]{:S(2)}) collective-permute-start(bf16[4,128,1024]{2,1,0:T(8,128)(2,1)} %fusion.29), channel_id=1, source_target_pairs={{0,4},{4,0},{1,5},{5,1},{2,6},{6,2},{3,7},{7,3},{8,12},{12,8},{9,1... | collective-permute-start | bytes 3145736 | tf_op jit(solution)/shard_map/ppermute | solution.py:69
  448.7 18.2 %all-to-all-start.5 = ((bf16[4,512,256]{2,1,0:T(8,128)(2,1)}), bf16[4,512,256]{2,1,0:T(8,128)(2,1)S(1)}, u32[]{:S(2)}, u32[]{:S(2)}) async-start(bf16[4,512,256]{2,1,0:T(8,128)(2,1)} %pad_maximum_fusion.2), calls=%async_computation.7 | async-start | bytes 2097152 | tf_op jit(solution)/shard_map/all_to_all | solution.py:463
  452.6 152.1 %reduce-scatter.10.cloned.1.call-start = ((), (), s32[]{:S(2)}) async-start(), calls=%async_computation.21 | async-start | bytes 2162688
  466.9 23.5 %all-to-all-start.8 = ((bf16[4,128,1024]{2,1,0:T(8,128)(2,1)}), bf16[4,128,1024]{2,1,0:T(8,128)(2,1)S(1)}, u32[]{:S(2)}, u32[]{:S(2)}) async-start(bf16[4,128,1024]{2,1,0:T(8,128)(2,1)} %fusion.13), calls=%async_computation.10 | async-start | bytes 2097152 | tf_op jit(solution)/shard_map/all_to_all | solution.py:86
  484.7 29.2 %collective-permute-start.4 = (bf16[4,128,512]{2,1,0:T(8,128)(2,1)}, bf16[4,128,512]{2,1,0:T(8,128)(2,1)}, u32[]{:S(2)}, u32[]{:S(2)}) collective-permute-start(bf16[4,128,512]{2,1,0:T(8,128)(2,1)} %fusion.48), channel_id=1, source_target_pairs={{0,4},{4,0},{1,5},{5,1},{2,6},{6,2},{3,7},{7,3},{8,12},{12,8},{9,1... | collective-permute-start | bytes 1572872 | tf_op jit(solution)/shard_map/ppermute | solution.py:69
  490.4 25.5 %all-to-all-start.7 = ((bf16[4,128,1024]{2,1,0:T(8,128)(2,1)}), bf16[4,128,1024]{2,1,0:T(8,128)(2,1)}, u32[]{:S(2)}, u32[]{:S(2)}) async-start(bf16[4,128,1024]{2,1,0:T(8,128)(2,1)} %fusion.14), calls=%async_computation.9 | async-start | bytes 2097152 | tf_op jit(solution)/shard_map/all_to_all | solution.py:86
  516.0 14.8 %all-to-all-start.6 = ((bf16[4,128,512]{2,1,0:T(8,128)(2,1)}), bf16[4,128,512]{2,1,0:T(8,128)(2,1)}, u32[]{:S(2)}, u32[]{:S(2)}) async-start(bf16[4,128,512]{2,1,0:T(8,128)(2,1)} %fusion.33), calls=%async_computation.8 | async-start | bytes 1048576 | tf_op jit(solution)/shard_map/all_to_all | solution.py:86
  530.8 78.1 %all-to-all-start.9 = ((bf16[16,32,678]{2,1,0:T(8,128)(2,1)}), bf16[16,32,678]{2,1,0:T(8,128)(2,1)S(1)}, u32[]{:S(2)}, u32[]{:S(2)}) async-start(bf16[16,32,678]{2,1,0:T(8,128)(2,1)} %fusion.21), calls=%async_computation.11 | async-start | bytes 1572864 | tf_op jit(solution)/shard_map/all_to_all | solution.py:86
  613.1 10.0 %all-to-all-start.10 = ((f32[32,1,2]{2,1,0:T(1,128)}), f32[32,1,2]{2,1,0:T(1,128)S(1)}, u32[]{:S(2)}, u32[]{:S(2)}) async-start(f32[32,1,2]{2,1,0:T(1,128)} %broadcast_in_dim.35), calls=%async_computation.12 | async-start | bytes 32768 | tf_op jit(solution)/shard_map/all_to_all | solution.py:93
  (81 other events, 657.3 us)
Sparse Core Ops, SparseCore 0:
  33.6 60.1 all-gather.5
  96.3 25.6 all-gather.9
  140.9 43.8 all-gather.7
  187.1 26.8 all-gather.11
  220.7 43.6 reduce-scatter.5
  271.8 44.8 all-gather.13
  326.6 42.4 reduce-scatter.7
  463.3 141.3 reduce-scatter.9

commit v2 on v1

--- a/solution.py
+++ b/solution.py
@@ -27,9 +27,10 @@
 STEP_RATES = (0.1, 0.2, 0.1, 0.05, 0.5, 0.5)
 LOG_TWO = 0.6931471805599453
 
-CHIPS = ("pair", "sub")
-SEQ = ("pair", "sub", "core")
-ALL = ("pair", "sub", "core", "ffn")
+CHIPS = ("p", "a", "b")
+SEQ = ("p", "a", "b", "core")
+ALL = ("p", "a", "b", "core", "ffn")
+GROUP = ("b", "core")
 F32 = jnp.float32
 BF16 = jnp.bfloat16
 
@@ -65,8 +66,12 @@
     return (weight - step_rate * change, new_one, new_two)
 
 
+def swap(values, axis):
+    return lax.ppermute(values, axis, [(0, 1), (1, 0)])
+
+
 def swap_core(values):
-    return lax.ppermute(values, "core", [(0, 1), (1, 0)])
+    return swap(values, "core")
 
 
 def spread_all(piece, axes):
@@ -85,6 +90,41 @@
     both = keep + swap_core(give.astype(BF16)).astype(F32)
     moved = lax.all_to_all(both.astype(BF16), axes, 0, 0, tiled=True)
     return jnp.sum(moved.astype(F32), axis=0)
+
+
+def group_rows(values):
+    near = jnp.stack([values, swap(values, "b")])
+    return jnp.concatenate([near, swap_core(near)]).reshape(-1, values.shape[1])
+
+
+def group_share(values):
+    parts = values.reshape(4, -1, values.shape[1])
+    near = parts[:2] + swap_core(parts[2:].astype(BF16)).astype(F32)
+    return near[0] + swap(near[1].astype(BF16), "b").astype(F32)
+
+
+def group_weight(pieces, n_ffn):
+    count, depth, hid = pieces.shape
+    moved = pieces.reshape(count, depth, 4, hid // 4).transpose(2, 0, 1, 3)
+    moved = lax.all_to_all(moved, GROUP, 0, 0, tiled=True)
+    whole = lax.all_gather(moved, ("ffn", "p", "a"), axis=0, tiled=False)
+    whole = whole.reshape(n_ffn, -1, count, depth, hid // 4).transpose(2, 1, 3, 0, 4)
+    return whole.reshape(count, -1, n_ffn * hid // 4)
+
+
+def group_scatter(grad, n_ffn, depth):
+    hid = grad.shape[1] // n_ffn
+    middle = lax.axis_size("a")
+    parts = grad.reshape(2, middle, 4 * depth, n_ffn, hid).transpose(0, 1, 3, 2, 4)
+    side = lax.axis_index("p")
+    keep = lax.dynamic_index_in_dim(parts, side, 0, keepdims=False)
+    give = lax.dynamic_index_in_dim(parts, 1 - side, 0, keepdims=False)
+    both = keep + swap(give.astype(BF16), "p").astype(F32)
+    both = both.astype(BF16).reshape(middle * n_ffn, 4, depth, hid)
+    moved = lax.all_to_all(both, ("a", "ffn"), 0, 0, tiled=True)
+    total = jnp.sum(moved.astype(F32), axis=0).astype(BF16)
+    back = lax.all_to_all(total, GROUP, 0, 0, tiled=True)
+    return back.astype(F32).transpose(1, 0, 2).reshape(depth, 4 * hid)
 
 
 def total_of(value):
@@ -272,6 +312,8 @@
 
 
 def per_device(
+    pair_axes,
+    half_axes,
     attn_in,
     attn_out,
     ffn_in,
@@ -296,12 +338,13 @@
     lengths,
     buckets,
 ):
-    pairs, subs, cores, n_ffn = (lax.axis_size(axis) for axis in ALL)
-    halves = subs * cores
+    n_ffn = lax.axis_size("ffn")
+    cores = lax.axis_size("core")
+    pairs, halves = lax.axis_size(pair_axes), lax.axis_size(half_axes)
     n_seq = pairs * halves
-    chips = pairs * subs
-    pair_rank = lax.axis_index("pair")
-    half_rank = lax.axis_index("sub") * cores + lax.axis_index("core")
+    chips = n_seq // cores
+    pair_rank = lax.axis_index(pair_axes)
+    half_rank = lax.axis_index(half_axes)
     seq_rank = pair_rank * halves + half_rank
     ffn_rank = lax.axis_index("ffn")
     num_seqs, seg_len = tokens.shape
@@ -317,7 +360,7 @@
     hid = ffn_in.shape[1]
 
     thin = jnp.concatenate([tables, norm_params], axis=0).astype(BF16).T
-    thin_all = spread_all(thin, ("pair", "sub", "ffn"))
+    thin_all = spread_all(thin, CHIPS + ("ffn",))
     thin_all = thin_all.reshape(chips, n_ffn, cores, slice_cols, thin.shape[1])
     thin_all = thin_all.transpose(0, 2, 1, 3, 4).reshape(width, thin.shape[1])
     table_all = thin_all[:, :rows_total]
@@ -326,8 +369,7 @@
     w_in = w_in.reshape(width, 2 * head_width)
     w_out = lax.all_gather(attn_out.astype(BF16).T, ("ffn",) + SEQ, axis=0, tiled=True)
     w_out = w_out.reshape(n_ffn, width, head_width)
-    w_up = lax.all_gather(ffn_in.astype(BF16), SEQ, axis=0, tiled=True)
-    w_down = lax.all_gather(ffn_out.astype(BF16).T, SEQ, axis=0, tiled=True)
+    w_up, w_down = group_weight(jnp.stack([ffn_in, ffn_out.T]).astype(BF16), n_ffn)
 
     seg_start = seq_rank * seg_len
     position = seg_start + jnp.arange(seg_len, dtype=jnp.int32)
@@ -353,12 +395,12 @@
     projected = mm(normed, w_in, PLAIN).astype(BF16)
     projected = projected.reshape(num_seqs, seg_len, 2, heads_local, HEAD)
     projected = projected.transpose(0, 3, 1, 2, 4).reshape(pairs, seg_len, 2 * HEAD)
-    own = lax.all_to_all(projected, "pair", 0, 0, tiled=True)
-    if subs == 1:
+    own = lax.all_to_all(projected, pair_axes, 0, 0, tiled=True)
+    if halves == cores:
         rows = jnp.stack([own, swap_core(own)])
         slots = jnp.arange(halves, dtype=jnp.int32) ^ half_rank
     else:
-        rows = lax.all_gather(own, ("sub", "core"), axis=0, tiled=False)
+        rows = lax.all_gather(own, half_axes, axis=0, tiled=False)
         slots = jnp.arange(halves, dtype=jnp.int32)
     info = jnp.concatenate([half_rank[None].astype(jnp.int32), slots.astype(jnp.int32)])
     my_seq = pair_rank // heads_local
@@ -369,7 +411,7 @@
     key_ids = jnp.where(usable[:, None], my_ids.T, -1).reshape(n_seq, seg_len, rounds)
     out, wide, stats, unit = attend(info, rows, key_ids, query_ids, rounds)
 
-    both = ("pair", "ffn")
+    both = pair_axes + ("ffn",)
     moved = lax.all_to_all(
         out.reshape(pairs * n_ffn, sub_len, HEAD), both, 0, 0, tiled=True
     )
@@ -377,24 +419,12 @@
     attended = moved.transpose(0, 3, 2, 1, 4).reshape(num_seqs * sub_len, n_ffn, head_width)
     branch = jnp.einsum("rzc,zdc->rd", attended, w_out, preferred_element_type=F32)
 
-    def whole_rows(values):
-        split = values.reshape(num_seqs, sub_len, -1)
-        return lax.all_gather(split, "ffn", axis=1, tiled=True).reshape(num_seqs * seg_len, -1)
-
-    def share_rows(values):
-        split = values.astype(BF16).reshape(num_seqs, seg_len, -1)
-        return (
-            lax.psum_scatter(split, "ffn", scatter_dimension=1, tiled=True)
-            .reshape(num_seqs * sub_len, -1)
-            .astype(F32)
-        )
-
     first_out = own_embed + branch
     middle_own, normal_two, inv_two = norm_forward(first_out, norm_rows[2], norm_rows[3])
-    middle = whole_rows(middle_own.astype(BF16))
+    middle = group_rows(middle_own.astype(BF16))
     pre_act = mm(middle, w_up, PLAIN)
     hidden = jnp.maximum(pre_act, 0.0).astype(BF16)
-    second_out = own_embed + share_rows(mm(hidden, w_down, CONTRACT_LAST))
+    second_out = own_embed + group_share(mm(hidden, w_down, CONTRACT_LAST))
     final_full, normal_three, inv_three = norm_forward(
         first_out + second_out, norm_rows[4], norm_rows[5]
     )
@@ -423,10 +453,10 @@
         grad_final, normal_three, inv_three, norm_rows[4]
     )
 
-    rows_grad = whole_rows(grad_sum.astype(BF16))
+    rows_grad = group_rows(grad_sum.astype(BF16))
     grad_hidden = mm(rows_grad, w_down, PLAIN)
     grad_pre = jnp.where(pre_act > 0.0, grad_hidden, 0.0).astype(BF16)
-    grad_middle = share_rows(mm(grad_pre, w_up, CONTRACT_LAST))
+    grad_middle = group_share(mm(grad_pre, w_up, CONTRACT_LAST))
     grad_down = mm(rows_grad, hidden, CONTRACT_FIRST)
     grad_up = mm(middle, grad_pre, CONTRACT_FIRST)
     first_part, gain_three, bias_three = norm_backward(
@@ -443,14 +473,14 @@
     query_grad, key_grad, value_grad = attend_back(
         info, rows, key_ids, query_ids, unit, grads, wide, stats, rounds
     )
-    if subs == 1:
+    if halves == cores:
         away = jnp.concatenate([key_grad[1], value_grad[1]], axis=-1).astype(BF16)
         came = swap_core(away).astype(F32)
         keys_total = key_grad[0] + came[..., :HEAD]
         values_total = value_grad[0] + came[..., HEAD:]
     else:
         away = jnp.concatenate([key_grad, value_grad], axis=-1).astype(BF16)
-        came = lax.psum_scatter(away, ("sub", "core"), scatter_dimension=0).astype(F32)
+        came = lax.psum_scatter(away, half_axes, scatter_dimension=0).astype(F32)
         keys_total, values_total = came[..., :HEAD], came[..., HEAD:]
     widened = own[..., :HEAD].astype(F32)
     inv_norm = lax.rsqrt(jnp.sum(widened * widened, axis=-1, keepdims=True) + KEY_EPS)
@@ -460,7 +490,7 @@
         - widened * inv_norm**3 * jnp.sum(widened * keys_total, axis=-1, keepdims=True)
     )
     owner_grads = jnp.concatenate([grad_qk, values_total], axis=-1).astype(BF16)
-    grad_proj = lax.all_to_all(owner_grads, "pair", 0, 0, tiled=True)
+    grad_proj = lax.all_to_all(owner_grads, pair_axes, 0, 0, tiled=True)
     grad_proj = grad_proj.reshape(num_seqs, heads_local, seg_len, 2, HEAD)
     grad_proj = grad_proj.transpose(0, 2, 3, 1, 4).reshape(num_seqs * seg_len, 2 * head_width)
     grad_in = mm(normed, grad_proj, CONTRACT_FIRST)
@@ -482,20 +512,17 @@
     thin_grad = jnp.concatenate([grad_tables, grad_norms], axis=1)
     thin_grad = thin_grad.reshape(chips, cores, n_ffn, slice_cols, -1).transpose(0, 2, 1, 3, 4)
     thin_grad = sum_scatter(
-        thin_grad.reshape(chips * n_ffn, cores, slice_cols, -1), ("pair", "sub", "ffn")
+        thin_grad.reshape(chips * n_ffn, cores, slice_cols, -1), CHIPS + ("ffn",)
     ).T
     table_grad, norm_grad = thin_grad[:rows_total], thin_grad[rows_total:]
     in_grad = sum_scatter(grad_in.reshape(chips, cores, -1, 2 * head_width), CHIPS)
     in_grad = in_grad.reshape(attn_in.shape)
-    out_grad = lax.psum_scatter(
-        grad_out.astype(BF16).reshape(n_ffn * width, head_width),
-        ("ffn",) + SEQ,
-        scatter_dimension=0,
-        tiled=True,
-    )
-    out_grad = out_grad.astype(F32).T
-    up_grad = sum_scatter(grad_up.reshape(chips, cores, -1, hid), CHIPS)
-    down_grad = sum_scatter(grad_down.reshape(chips, cores, -1, hid), CHIPS).T
+    out_grad = grad_out.reshape(n_ffn, chips, cores, -1, head_width).transpose(1, 0, 2, 3, 4)
+    out_grad = sum_scatter(
+        out_grad.reshape(chips * n_ffn, cores, -1, head_width), CHIPS + ("ffn",)
+    ).T
+    up_grad = group_scatter(grad_up, n_ffn, ffn_in.shape[0])
+    down_grad = group_scatter(grad_down, n_ffn, ffn_in.shape[0]).T
 
     grad_list = (in_grad, out_grad, up_grad, down_grad, table_grad, norm_grad)
     local_sq = jnp.float32(0.0)
@@ -530,8 +557,13 @@
 
     def step(*args):
         num_pairs = args[18].shape[0] * (args[0].shape[2] // HEAD // n_ffn)
-        subs = n_seq // 2 // num_pairs
-        fine = Mesh(mesh.devices.reshape(num_pairs, subs, 2, n_ffn), ALL)
+        fine = Mesh(mesh.devices.reshape(2, n_seq // 8, 2, 2, n_ffn), ALL)
+        if num_pairs == n_seq // 2:
+            pair_axes, half_axes = CHIPS, ("core",)
+        elif num_pairs == 2:
+            pair_axes, half_axes = ("p",), ("a", "b", "core")
+        else:
+            raise ValueError(num_pairs)
         weights = (
             P(SEQ, None, "ffn"),
             P("ffn", SEQ),
@@ -541,7 +573,7 @@
             P(None, ALL),
         )
         return jax.shard_map(
-            per_device,
+            functools.partial(per_device, pair_axes, half_axes),
             mesh=fine,
             in_specs=weights * 3 + (P(None, SEQ), P(None, ALL), P(), P(), P()),
             out_specs=weights * 3 + (P(), P()),

time: 663 us -> 565 us (0.85)
  waiting for transfers between devices: 316 us -> 194 us
  local copies, waits for them, and re-layouts: 91 us -> 115 us
  starting transfers between devices: 53 us -> 70.3 us
  matrix products: 57.3 us -> 42.5 us
    all_gather x4 -> x1, waiting for transfers between devices: 110 us -> 0.01 us  [group_weight(): whole = lax.all_gather(moved, ('ffn', 'p', 'a'), axis=0, tiled=False)]
    reduce_scatter x2 -> x0, waiting for transfers between devices: 74.6 us -> none  [share_rows(): lax.psum_scatter(split, 'ffn', scatter_dimension=1, tiled=True)]
    unnamed x9 -> x2, waiting for transfers between devices: 63.4 us -> 0.03 us
    ppermute x8 -> x17, waiting for transfers between devices: 0.08 us -> 59.6 us  [swap(): return lax.ppermute(values, axis, [(0, 1), (1, 0)])]
    all_to_all x2 -> x7, waiting for transfers between devices: 20.6 us -> 46.7 us  [the longest x1 17.5 us: per_device(): own = lax.all_to_all(projected, pair_axes, 0, 0, tiled=True)]
    all_to_all x2 -> x7, starting transfers between devices: 7.55 us -> 26.9 us  [the longest x2 8.66 us: group_scatter(): moved = lax.all_to_all(both, ('a', 'ffn'), 0, 0, tiled=True)]
    all_to_all x1, waiting for transfers between devices: 10.6 us -> 26 us  [per_device(): lax.all_to_all(out.reshape(pairs * n_ffn, sub_len, HEAD), both, 0, 0, til...]
    dot_general x14, matrix products: 51.9 us -> 37.7 us  [mm(): return lax.dot_general(left, right, dims, preferred_element_type=F32)]
  transfers between devices with their start and end apart: 27 -> 34, of which waited for: 15 -> 20; matrix products, arithmetic and copies ran while one was open for 23% -> 27% of each run, Pallas kernels for 3% -> 8%
where the time goes in v2:
time: 565 us; the launch traced here: 555 us
  waiting for transfers between devices  194 us (34%)
  local copies, waits for them, and re-layouts  115 us (20%)
  starting transfers between devices  70.3 us (12%)
  other arithmetic  69.9 us (12%)
  matrix products  42.5 us (8%)
  Pallas kernels  42.4 us (8%)
  between operations  21.7 us (4%)
    ppermute x17, waiting for transfers between devices, swap(): return lax.ppermute(values, axis, [(0, 1), (1, 0)])  59.6 us
    dot_general x14, matrix products, mm(): return lax.dot_general(left, right, dims, preferred_element_type=F32)  37.7 us
    all_to_all x2, waiting for transfers between devices, spread_all(): own = lax.all_to_all(copies, axes, 0, 0, tiled=True)  31.5 us
    unnamed x162, local copies, waits for them, and re-layouts  28.9 us
    all_to_all x1, waiting for transfers between devices, per_device(): lax.all_to_all(out.reshape(pairs * n_ffn, sub_len, HEAD), both, 0, 0, til...  26 us
    pallas_call x1, Pallas kernels, attend_back(): pl.pallas_call(functools.partial(backward_kernel, rounds), out_shape=(jax...  22.5 us
    pallas_call x1, Pallas kernels, attend(): pl.pallas_call(functools.partial(forward_kernel, rounds), out_shape=(jax....  19.9 us
    all_to_all x3, waiting for transfers between devices, sum_scatter(): moved = lax.all_to_all(both.astype(BF16), axes, 0, 0, tiled=True)  17.9 us
  transfers between devices with their start and end apart: 34, of which 20 were waited for; matrix products, arithmetic and copies ran while one was open for 27% of the time, Pallas kernels for 8%

profile of v2, /device:TPU:0, one launch (start us, length us, event | category | flops | bytes accessed | tf_op | source)
XLA Modules:
  0.0 555.3 jit_solution(14589337532300041275)
XLA Ops:
  10.7 5.2 all-to-all-start.1
  16.2 7.8 %all-to-all-done.1 = bf16[4,128,512]{2,1,0:T(8,128)(2,1)S(1)} async-done(((bf16[4,128,512]{2,1,0:T(8,128)(2,1)}), bf16[4,128,512]{2,1,0:T(8,128)(2,1)S(1)}, u32[]{:S(2)}, u32[]{:S(2)}) %all-to-all-start.1) | async-done | bytes 524320 | tf_op jit(solution)/shard_map/all_to_all | solution.py:80
  24.9 5.9 %all-to-all-start = ((bf16[16,32,678]{2,1,0:T(8,128)(2,1)}), bf16[16,32,678]{2,1,0:T(8,128)(2,1)S(1)}, u32[]{:S(2)}, u32[]{:S(2)}) async-start(bf16[16,32,678]{2,1,0:T(8,128)(2,1)} %broadcast_in_dim.27), calls=%async_computation | async-start | bytes 1572864 | tf_op jit(solution)/shard_map/all_to_all | solution.py:80
  32.0 23.7 %all-to-all-done = bf16[16,32,678]{2,1,0:T(8,128)(2,1)S(1)} async-done(((bf16[16,32,678]{2,1,0:T(8,128)(2,1)}), bf16[16,32,678]{2,1,0:T(8,128)(2,1)S(1)}, u32[]{:S(2)}, u32[]{:S(2)}) %all-to-all-start) | async-done | bytes 694304 | tf_op jit(solution)/shard_map/all_to_all | solution.py:80
  60.4 8.0 %all-to-all-done.4 = bf16[4,2,128,256]{2,3,1,0:T(8,128)(2,1)S(1)} async-done(((bf16[4,2,128,256]{2,3,1,0:T(8,128)(2,1)}), bf16[4,2,128,256]{2,3,1,0:T(8,128)(2,1)S(1)}, u32[]{:S(2)}, u32[]{:S(2)}) %all-to-all-start.4) | async-done | bytes 524320 | tf_op jit(solution)/shard_map/all_to_all | solution.py:109
  85.4 17.5 %all-to-all-done.2 = bf16[4,512,256]{2,1,0:T(8,128)(2,1)S(1)} async-done(((bf16[4,512,256]{2,1,0:T(8,128)(2,1)}), bf16[4,512,256]{2,1,0:T(8,128)(2,1)S(1)}, u32[]{:S(2)}, u32[]{:S(2)}) %all-to-all-start.2) | async-done | bytes 1048608 | tf_op jit(solution)/shard_map/all_to_all | solution.py:398
  107.1 19.9 %attend.1 = (bf16[4,512,128]{2,1,0:T(8,128)(2,1)}, f32[4,512,128]{2,1,0:T(8,128)}, f32[4,2,512]{2,1,0:T(2,128)}, bf16[2,4,512,128]{3,2,1,0:T(8,128)(2,1)}) custom-call(s32[3]{0:T(128)} %pad_add_fusion.info_ref, bf16[2,4,512,256]{3,2,1,0:T(8,128)(2,1)} %pad_maximum_fusion.rows_ref, s32[8,512,2]{2,1,0:T(8,128)} %bitcast.309, s32[8,2,512]{2,1,0:T(2,128)} %bitcast.372), custom_call_target="tpu_custom_call" | custom-call | tf_op jit(solution)/shard_map/attend/pallas_call | solution.py:283
  127.0 5.7 %all-to-all-start.3 = ((bf16[16,128,128]{2,1,0:T(8,128)(2,1)}), bf16[16,128,128]{2,1,0:T(8,128)(2,1)S(1)}, u32[]{:S(2)}, u32[]{:S(2)}) async-start(bf16[16,128,128]{2,1,0:T(8,128)(2,1)} %bitcast.371), calls=%async_computation.3 | async-start | bytes 1048576 | tf_op jit(solution)/shard_map/all_to_all | solution.py:415
  138.1 26.0 %all-to-all-done.3 = bf16[16,128,128]{2,1,0:T(8,128)(2,1)S(1)} async-done(((bf16[16,128,128]{2,1,0:T(8,128)(2,1)}), bf16[16,128,128]{2,1,0:T(8,128)(2,1)S(1)}, u32[]{:S(2)}, u32[]{:S(2)}) %all-to-all-start.3) | async-done | bytes 524320 | tf_op jit(solution)/shard_map/all_to_all | solution.py:415
  169.3 14.3 %collective-permute-done.3 = bf16[256,1024]{1,0:T(8,128)(2,1)S(1)} collective-permute-done((bf16[256,1024]{1,0:T(8,128)(2,1)S(1)}, bf16[256,1024]{1,0:T(8,128)(2,1)S(1)}, u32[]{:S(2)}, u32[]{:S(2)}) %collective-permute-start.3) | collective-permute-done | bytes 524320 | tf_op jit(solution)/shard_map/ppermute | solution.py:70
  201.7 6.7 %maximum_convert_fusion = (bf16[1024,1024]{0,1:T(8,128)(2,1)S(1)}, f32[1024,1024]{0,1:T(8,128)}) fusion(bf16[1024,1024]{1,0:T(8,128)(2,1)} %bitcast.322, bf16[128,8,8,128]{3,2,1,0:T(8,128)(2,1)} %bitcast.345), kind=kOutput, calls=%fused_computation.5 | convolution fusion | flops 2149580800 | bytes 10485760 | tf_op jit(solution)/shard_map/dot_general | solution.py:142
  216.8 13.9 %collective-permute-done.6 = bf16[256,1024]{1,0:T(8,128)(2,1)} collective-permute-done((bf16[256,1024]{1,0:T(8,128)(2,1)}, bf16[256,1024]{1,0:T(8,128)(2,1)}, u32[]{:S(2)}, u32[]{:S(2)}) %collective-permute-start.6) | collective-permute-done | bytes 524320 | tf_op jit(solution)/shard_map/ppermute | solution.py:70
  237.4 12.8 %collective-permute-done.7 = bf16[256,1024]{1,0:T(8,128)(2,1)S(1)} collective-permute-done((bf16[256,1024]{1,0:T(8,128)(2,1)S(1)}, bf16[256,1024]{1,0:T(8,128)(2,1)S(1)}, u32[]{:S(2)}, u32[]{:S(2)}) %collective-permute-start.7) | collective-permute-done | bytes 524320 | tf_op jit(solution)/shard_map/ppermute | solution.py:70
  275.6 9.5 %collective-permute-done.10 = bf16[256,1024]{1,0:T(8,128)(2,1)S(1)} collective-permute-done((bf16[256,1024]{1,0:T(8,128)(2,1)S(1)}, bf16[256,1024]{1,0:T(8,128)(2,1)S(1)}, u32[]{:S(2)}, u32[]{:S(2)}) %collective-permute-start.10) | collective-permute-done | bytes 524320 | tf_op jit(solution)/shard_map/ppermute | solution.py:70
  305.0 9.0 %all-to-all-done.5 = bf16[16,128,128]{2,1,0:T(8,128)(2,1)} async-done(((bf16[16,128,128]{2,1,0:T(8,128)(2,1)}), bf16[16,128,128]{2,1,0:T(8,128)(2,1)}, u32[]{:S(2)}, u32[]{:S(2)}) %all-to-all-start.5) | async-done | bytes 524320 | tf_op jit(solution)/shard_map/all_to_all | solution.py:472
  325.8 22.5 %attend_back.1 = (f32[4,512,128]{2,1,0:T(8,128)}, f32[2,4,512,128]{3,2,1,0:T(8,128)}, f32[2,4,512,128]{3,2,1,0:T(8,128)}) custom-call(s32[3]{0:T(128)} %pad_add_fusion.info_ref, bf16[2,4,512,256]{3,2,1,0:T(8,128)(2,1)} %pad_maximum_fusion.rows_ref, s32[8,512,2]{2,1,0:T(8,128)} %bitcast.310, s32[8,2,512]{2,1,0:T(2,128)} %bitcast.373, ...), custom_call_target="tpu_custom_call" | custom-call | tf_op jit(solution)/shard_map/attend_back/pallas_call | solution.py:300
  357.7 5.1 all-to-all-start.9
  373.6 15.2 %all-to-all-done.9 = bf16[4,4,128,256]{3,2,1,0:T(8,128)(2,1)} async-done(((bf16[4,4,128,256]{3,2,1,0:T(8,128)(2,1)}), bf16[4,4,128,256]{3,2,1,0:T(8,128)(2,1)}, u32[]{:S(2)}, u32[]{:S(2)}) %all-to-all-start.9) | async-done | bytes 1048608 | tf_op jit(solution)/shard_map/all_to_all | solution.py:124
  418.8 6.5 %multiply_reduce_fusion = (f32[1024]{0:T(1024)S(1)}, f32[1024]{0:T(1024)S(1)}, f32[1024]{0:T(1024)S(1)}, f32[1024]{0:T(1024)S(1)}, f32[1024,1024]{1,0:T(8,128)}) fusion(f32[1024,1024]{1,0:T(8,128)} %copy-done, f32[1024]{0:T(1024)S(1)} %add_rsqrt_fusion.1, f32[1024]{0:T(1024)S(1)} %broadcast_multiply_fusion.3, f32[1024]{0:T(1024)S(1)} %get-tuple-element.251, ...), kind=kOutput, calls=%fused_computation.1 | convolution fusion | flops 1083174912 | bytes 10514432 | tf_op jit(solution)/shard_map/dot_general | solution.py:142
  431.5 6.0 %all-to-all-done.10 = bf16[4,128,256]{2,1,0:T(8,128)(2,1)S(1)} async-done(((bf16[4,128,256]{2,1,0:T(8,128)(2,1)}), bf16[4,128,256]{2,1,0:T(8,128)(2,1)S(1)}, u32[]{:S(2)}, u32[]{:S(2)}) %all-to-all-start.10) | async-done | bytes 262176 | tf_op jit(solution)/shard_map/all_to_all | solution.py:126
  455.7 5.9 %concatenate.58 = f32[4,2,4,32,678]{4,3,2,1,0:T(8,128)} concatenate(f32[4,2,4,32,672]{4,3,2,1,0:T(8,128)S(1)} %bitcast.314, f32[4,2,4,32,1]{4,3,2,1,0:T(8,128)} %concatenate.59, f32[4,2,4,32,1]{4,3,2,1,0:T(8,128)} %concatenate.60, f32[4,2,4,32,1]{4,3,2,1,0:T(8,128)} %concatenate.61, f32[4,2,4,32,1]{4,3,2,1,0:T(8,128)} %concatenate.62, f32[4,2,4,32,1]{4,3,2,1,0:T(8,128)} %concatenate.63, ...), dimensions={4} | concatenate | bytes 5554176 | tf_op jit(solution)/shard_map/concatenate | solution.py:512
  476.0 5.0 all-to-all-done.7
  481.0 4.9 all-to-all-start.13
  497.4 10.2 %all-to-all-done.13 = bf16[16,32,678]{2,1,0:T(8,128)(2,1)S(1)} async-done(((bf16[16,32,678]{2,1,0:T(8,128)(2,1)}), bf16[16,32,678]{2,1,0:T(8,128)(2,1)S(1)}, u32[]{:S(2)}, u32[]{:S(2)}) %all-to-all-start.13) | async-done | bytes 694304 | tf_op jit(solution)/shard_map/all_to_all | solution.py:91
  (376 shorter events, 266.4 us)
Async XLA Ops:
  7.2 126.8 %all-gather.4.cloned.1.call-start = ((), (), s32[]{:S(2)}) async-start(), calls=%async_computation.15 | async-start | bytes 2162688 | tf_op jit(solution)/shard_map/all_gather | solution.py:370
  10.7 13.2 %all-to-all-start.1 = ((bf16[4,128,512]{2,1,0:T(8,128)(2,1)}), bf16[4,128,512]{2,1,0:T(8,128)(2,1)S(1)}, u32[]{:S(2)}, u32[]{:S(2)}) async-start(bf16[4,128,512]{2,1,0:T(8,128)(2,1)} %broadcast_in_dim.30), calls=%async_computation.1 | async-start | bytes 1048576 | tf_op jit(solution)/shard_map/all_to_all | solution.py:80
  24.9 30.8 %all-to-all-start = ((bf16[16,32,678]{2,1,0:T(8,128)(2,1)}), bf16[16,32,678]{2,1,0:T(8,128)(2,1)S(1)}, u32[]{:S(2)}, u32[]{:S(2)}) async-start(bf16[16,32,678]{2,1,0:T(8,128)(2,1)} %broadcast_in_dim.27), calls=%async_computation | async-start | bytes 1572864 | tf_op jit(solution)/shard_map/all_to_all | solution.py:80
  32.0 37.4 %collective-permute-start.1 = (bf16[4,128,512]{2,1,0:T(8,128)(2,1)S(1)}, bf16[4,128,512]{2,1,0:T(8,128)(2,1)}, u32[]{:S(2)}, u32[]{:S(2)}) collective-permute-start(bf16[4,128,512]{2,1,0:T(8,128)(2,1)S(1)} %all-to-all-done.1), channel_id=1, source_target_pairs={{0,4},{4,0},{1,5},{5,1},{2,6},{6,2},{3,7},{7,3},{8,12},{12,8},{9,1... | collective-permute-start | bytes 1572872 | tf_op jit(solution)/shard_map/ppermute | solution.py:70
  55.8 12.6 %all-to-all-start.4 = ((bf16[4,2,128,256]{2,3,1,0:T(8,128)(2,1)}), bf16[4,2,128,256]{2,3,1,0:T(8,128)(2,1)S(1)}, u32[]{:S(2)}, u32[]{:S(2)}) async-start(bf16[4,2,128,256]{2,3,1,0:T(8,128)(2,1)} %copy.402), calls=%async_computation.4 | async-start | bytes 1048576 | tf_op jit(solution)/shard_map/all_to_all | solution.py:109
  59.2 128.7 %all-gather.6.cloned.1.call-start = ((), (), s32[]{:S(2)}) async-start(), calls=%async_computation.16 | async-start | bytes 4718592 | tf_op jit(solution)/shard_map/all_gather | solution.py:110
  79.7 23.2 %all-to-all-start.2 = ((bf16[4,512,256]{2,1,0:T(8,128)(2,1)}), bf16[4,512,256]{2,1,0:T(8,128)(2,1)S(1)}, u32[]{:S(2)}, u32[]{:S(2)}) async-start(bf16[4,512,256]{2,1,0:T(8,128)(2,1)} %reshape.452), calls=%async_computation.2 | async-start | bytes 2097152 | tf_op jit(solution)/shard_map/all_to_all | solution.py:398
  127.0 37.2 %all-to-all-start.3 = ((bf16[16,128,128]{2,1,0:T(8,128)(2,1)}), bf16[16,128,128]{2,1,0:T(8,128)(2,1)S(1)}, u32[]{:S(2)}, u32[]{:S(2)}) async-start(bf16[16,128,128]{2,1,0:T(8,128)(2,1)} %bitcast.371), calls=%async_computation.3 | async-start | bytes 1048576 | tf_op jit(solution)/shard_map/all_to_all | solution.py:415
  169.0 14.6 %collective-permute-start.3 = (bf16[256,1024]{1,0:T(8,128)(2,1)S(1)}, bf16[256,1024]{1,0:T(8,128)(2,1)S(1)}, u32[]{:S(2)}, u32[]{:S(2)}) collective-permute-start(bf16[256,1024]{1,0:T(8,128)(2,1)S(1)} %add_convert_fusion.2), channel_id=1, source_target_pairs={{0,8},{8,0},{1,9},{9,1},{2,10},{10,2},{3,11},{11,3},{4,12},{12,4},... | collective-permute-start | bytes 1572872 | tf_op jit(solution)/shard_map/ppermute | solution.py:70
  216.4 14.3 %collective-permute-start.6 = (bf16[256,1024]{1,0:T(8,128)(2,1)}, bf16[256,1024]{1,0:T(8,128)(2,1)}, u32[]{:S(2)}, u32[]{:S(2)}) collective-permute-start(bf16[256,1024]{1,0:T(8,128)(2,1)} %fusion.60), channel_id=1, source_target_pairs={{0,8},{8,0},{1,9},{9,1},{2,10},{10,2},{3,11},{11,3},{4,12},{12,4},... | collective-permute-start | bytes 1572872 | tf_op jit(solution)/shard_map/ppermute | solution.py:70
  237.1 13.1 %collective-permute-start.7 = (bf16[256,1024]{1,0:T(8,128)(2,1)S(1)}, bf16[256,1024]{1,0:T(8,128)(2,1)S(1)}, u32[]{:S(2)}, u32[]{:S(2)}) collective-permute-start(bf16[256,1024]{1,0:T(8,128)(2,1)S(1)} %get-tuple-element.274), channel_id=1, source_target_pairs={{0,8},{8,0},{1,9},{9,1},{2,10},{10,2},{3,11},{11,3},{4,12},{12,4},... | collective-permute-start | bytes 1572872 | tf_op jit(solution)/shard_map/ppermute | solution.py:70
  270.8 14.3 %collective-permute-start.10 = (bf16[256,1024]{1,0:T(8,128)(2,1)S(1)}, bf16[256,1024]{1,0:T(8,128)(2,1)S(1)}, u32[]{:S(2)}, u32[]{:S(2)}) collective-permute-start(bf16[256,1024]{1,0:T(8,128)(2,1)S(1)} %fusion.61), channel_id=1, source_target_pairs={{0,8},{8,0},{1,9},{9,1},{2,10},{10,2},{3,11},{11,3},{4,12},{12,4},... | collective-permute-start | bytes 1572872 | tf_op jit(solution)/shard_map/ppermute | solution.py:70
  275.1 26.8 %collective-permute-start.15 = (bf16[1,4,512,256]{3,2,1,0:T(8,128)(2,1)}, bf16[1,4,512,256]{3,2,1,0:T(8,128)(2,1)}, u32[]{:S(2)}, u32[]{:S(2)}) collective-permute-start(bf16[1,4,512,256]{3,2,1,0:T(8,128)(2,1)} %fusion.42), channel_id=1, source_target_pairs={{0,16},{16,0},{1,17},{17,1},{2,18},{18,2},{3,19},{19,3},{4,20},{20... | collective-permute-start | bytes 3145736 | tf_op jit(solution)/shard_map/ppermute | solution.py:70
  293.5 20.5 %all-to-all-start.5 = ((bf16[16,128,128]{2,1,0:T(8,128)(2,1)}), bf16[16,128,128]{2,1,0:T(8,128)(2,1)}, u32[]{:S(2)}, u32[]{:S(2)}) async-start(bf16[16,128,128]{2,1,0:T(8,128)(2,1)} %bitcast.353), calls=%async_computation.5 | async-start | bytes 1048576 | tf_op jit(solution)/shard_map/all_to_all | solution.py:472
  314.0 43.6 %all-to-all-start.11 = ((bf16[4,4,128,256]{3,2,1,0:T(8,128)(2,1)}), bf16[4,4,128,256]{3,2,1,0:T(8,128)(2,1)S(1)}, u32[]{:S(2)}, u32[]{:S(2)}) async-start(bf16[4,4,128,256]{3,2,1,0:T(8,128)(2,1)} %bitcast.100), calls=%async_computation.11 | async-start | bytes 2097152 | tf_op jit(solution)/shard_map/all_to_all | solution.py:124
  325.2 29.8 %collective-permute-start.14 = (bf16[1,4,512,256]{3,2,1,0:T(8,128)(2,1)}, bf16[1,4,512,256]{3,2,1,0:T(8,128)(2,1)}, u32[]{:S(2)}, u32[]{:S(2)}) collective-permute-start(bf16[1,4,512,256]{3,2,1,0:T(8,128)(2,1)} %fusion.41), channel_id=1, source_target_pairs={{0,16},{16,0},{1,17},{17,1},{2,18},{18,2},{3,19},{19,3},{4,20},{20... | collective-permute-start | bytes 3145736 | tf_op jit(solution)/shard_map/ppermute | solution.py:70
  352.2 13.5 %collective-permute-start.11 = (bf16[4,512,256]{2,1,0:T(8,128)(2,1)}, bf16[4,512,256]{2,1,0:T(8,128)(2,1)}, u32[]{:S(2)}, u32[]{:S(2)}) collective-permute-start(bf16[4,512,256]{2,1,0:T(8,128)(2,1)} %pad_maximum_fusion.5), channel_id=1, source_target_pairs={{0,4},{4,0},{1,5},{5,1},{2,6},{6,2},{3,7},{7,3},{8,12},{12,8},{9,1... | collective-permute-start | bytes 3145736 | tf_op jit(solution)/shard_map/ppermute | solution.py:70
  357.7 31.1 %all-to-all-start.9 = ((bf16[4,4,128,256]{3,2,1,0:T(8,128)(2,1)}), bf16[4,4,128,256]{3,2,1,0:T(8,128)(2,1)}, u32[]{:S(2)}, u32[]{:S(2)}) async-start(bf16[4,4,128,256]{3,2,1,0:T(8,128)(2,1)} %bitcast.86), calls=%async_computation.9 | async-start | bytes 2097152 | tf_op jit(solution)/shard_map/all_to_all | solution.py:124
  365.7 41.9 %collective-permute-start.13 = (bf16[16,128,256]{2,1,0:T(8,128)(2,1)}, bf16[16,128,256]{2,1,0:T(8,128)(2,1)}, u32[]{:S(2)}, u32[]{:S(2)}) collective-permute-start(bf16[16,128,256]{2,1,0:T(8,128)(2,1)} %fusion.40), channel_id=1, source_target_pairs={{0,4},{4,0},{1,5},{5,1},{2,6},{6,2},{3,7},{7,3},{8,12},{12,8},{9,1... | collective-permute-start | bytes 3145736 | tf_op jit(solution)/shard_map/ppermute | solution.py:70
  388.8 21.9 %all-to-all-start.6 = ((bf16[4,512,256]{2,1,0:T(8,128)(2,1)}), bf16[4,512,256]{2,1,0:T(8,128)(2,1)}, u32[]{:S(2)}, u32[]{:S(2)}) async-start(bf16[4,512,256]{2,1,0:T(8,128)(2,1)} %pad_maximum_fusion.6), calls=%async_computation.6 | async-start | bytes 2097152 | tf_op jit(solution)/shard_map/all_to_all | solution.py:493
  410.7 17.4 %all-to-all-start.12 = ((bf16[4,128,256]{2,1,0:T(8,128)(2,1)}), bf16[4,128,256]{2,1,0:T(8,128)(2,1)S(1)}, u32[]{:S(2)}, u32[]{:S(2)}) async-start(bf16[4,128,256]{2,1,0:T(8,128)(2,1)} %reduce_sum.352), calls=%async_computation.12 | async-start | bytes 524288 | tf_op jit(solution)/shard_map/all_to_all | solution.py:126
  427.5 37.4 %collective-permute-start.12 = (bf16[4,128,512]{2,1,0:T(8,128)(2,1)}, bf16[4,128,512]{2,1,0:T(8,128)(2,1)}, u32[]{:S(2)}, u32[]{:S(2)}) collective-permute-start(bf16[4,128,512]{2,1,0:T(8,128)(2,1)} %fusion.59), channel_id=1, source_target_pairs={{0,4},{4,0},{1,5},{5,1},{2,6},{6,2},{3,7},{7,3},{8,12},{12,8},{9,1... | collective-permute-start | bytes 1572872 | tf_op jit(solution)/shard_map/ppermute | solution.py:70
  437.5 32.1 %all-to-all-start.8 = ((bf16[16,128,256]{2,1,0:T(8,128)(2,1)}), bf16[16,128,256]{2,1,0:T(8,128)(2,1)}, u32[]{:S(2)}, u32[]{:S(2)}) async-start(bf16[16,128,256]{2,1,0:T(8,128)(2,1)} %fusion.19), calls=%async_computation.8 | async-start | bytes 2097152 | tf_op jit(solution)/shard_map/all_to_all | solution.py:91
  481.0 26.5 %all-to-all-start.13 = ((bf16[16,32,678]{2,1,0:T(8,128)(2,1)}), bf16[16,32,678]{2,1,0:T(8,128)(2,1)S(1)}, u32[]{:S(2)}, u32[]{:S(2)}) async-start(bf16[16,32,678]{2,1,0:T(8,128)(2,1)} %fusion.32), calls=%async_computation.13 | async-start | bytes 1572864 | tf_op jit(solution)/shard_map/all_to_all | solution.py:91
  (81 other events, 520.8 us)
Sparse Core Ops, SparseCore 0:
  11.4 62.7 all-gather.3
  76.9 88.7 all-gather.5
